TPU v7x, 256 devices: a whole 4x4x8 slice. The times are simulated.
256 devices in a mesh: order: 8 (over y, core), basin: 32 (over z, x).
Axes of the slice: x: 4, y: 4, z: 8, core: 2. Of those that a mesh axis runs over, the one named last changes fastest.
Arguments:
- forcings: bfloat16 [32, 16, 131072], P(None, None, ('order', 'basin')), may hold values from -6 to 6
- w_input: bfloat16 [512, 16], replicated, may hold values from -1.5 to 1.5
- w_recur: bfloat16 [512, 128], replicated, may hold values from -0.5 to 0.5
- gate_bias: float32 [512], replicated, may hold values from -3 to 3
- w_runoff: float32 [128], replicated, may hold values from -0.5 to 0.5
- travel_time: float32 [131072], P(('order', 'basin')), may hold values from 1 to 8
- weight_x: float32 [131072], P(('order', 'basin')), may hold values from 0 to 0.3
- drain_basin: int32 [131072, 1], P(('order', 'basin')), may hold values from 0 to 31; in each aligned block of 512 rows (0 to 511, 512 to 1023, ...) at most 32 rows name the same one
- drain_reach: int32 [131072, 1], P(('order', 'basin')), may hold values from 0 to 511
Outputs:
- discharge: float32 [32, 131072], P(None, ('order', 'basin'))
Inputs may be any that keep to these rules, and one draw needn't show every extreme that they name: `drain_basin`: among the reaches of one device (aligned blocks of 512 reaches), at most 32 drain to the same basin index, and exactly 32 do for some basin index in some block.
All inputs are finite; a program needn't handle non-finite values.
Results may differ from a plain program's by a relative error of at most 0.0003.
Values sent between devices are 32-bit elements; how exact they have to be, the bound alone decides.
A program may use at most 64 MiB of HBM per device.

v0:
```python
import functools

import jax
import jax.numpy as jnp
from jax import lax
from jax.experimental import pallas as pl
from jax.experimental.pallas import tpu as pltpu
from jax.sharding import PartitionSpec as P

MESH = pl.DeviceIdType.MESH


def lstm_days(lstm_state, day_block, w_input, w_recur, gate_bias, w_runoff):
    units = w_recur.shape[1]

    def one_day(recurrent, inputs):
        hidden, memory = recurrent
        gate_sums = (
            jnp.dot(w_input, inputs, preferred_element_type=jnp.float32)
            + jnp.dot(w_recur, hidden, preferred_element_type=jnp.float32)
            + gate_bias[:, None]
        )
        ingate = jax.nn.sigmoid(gate_sums[:units])
        forget = jax.nn.sigmoid(gate_sums[units : 2 * units])
        candidate = jnp.tanh(gate_sums[2 * units : 3 * units])
        outgate = jax.nn.sigmoid(gate_sums[3 * units :])
        memory = forget * memory + ingate * candidate
        hidden = (outgate * jnp.tanh(memory)).astype(jnp.bfloat16)
        runoff = jax.nn.softplus(
            jnp.dot(w_runoff, hidden.astype(jnp.float32), precision=lax.Precision.HIGHEST)
        )
        return ((hidden, memory), runoff)

    return lax.scan(one_day, lstm_state, day_block)


def split3(x):
    hi = x.astype(jnp.bfloat16)
    rest = x - hi.astype(jnp.float32)
    mid = rest.astype(jnp.bfloat16)
    lo = (rest - mid.astype(jnp.float32)).astype(jnp.bfloat16)
    return hi, mid, lo


def chain_kernel(n_order, n_basin, cap, runoff_ref, coef_ref, send_ref, table_ref, out_ref,
                 packed, recv, send_sem, recv_sem):
    o = lax.axis_index("order")
    b = lax.axis_index("basin")
    days = runoff_ref.shape[0]

    barrier = pltpu.get_barrier_semaphore()

    def greet(row):
        def body(j, carry):
            pl.semaphore_signal(barrier, inc=1, device_id=(row, j), device_id_type=MESH)
            return carry
        lax.fori_loop(0, n_basin, body, 0)

    @pl.when(o > 0)
    def _():
        greet(o - 1)

    @pl.when(o < n_order - 1)
    def _():
        greet(o + 1)

    at_end = jnp.logical_or(o == 0, o == n_order - 1)

    @pl.when(at_end)
    def _():
        pl.semaphore_wait(barrier, n_basin)

    @pl.when(jnp.logical_not(at_end))
    def _():
        pl.semaphore_wait(barrier, 2 * n_basin)

    out_ref[...] = runoff_ref[...]

    @pl.when(o > 0)
    def _():
        def arrived(j, carry):
            pltpu.make_async_remote_copy(
                src_ref=packed.at[pl.ds(j * cap, cap)],
                dst_ref=recv.at[pl.ds(j * cap, cap)],
                send_sem=send_sem.at[j],
                recv_sem=recv_sem.at[j],
                device_id=(o - 1, j),
                device_id_type=MESH,
            ).wait_recv()
            return carry
        lax.fori_loop(0, n_basin, arrived, 0)
        arrive = None
        for part in split3(recv[...]):
            term = lax.dot_general(part, table_ref[...], (((0,), (0,)), ((), ())),
                                   preferred_element_type=jnp.float32)
            arrive = term if arrive is None else arrive + term
        out_ref[...] = out_ref[...] + arrive

    inflow = out_ref[...]
    c0 = coef_ref[0:1, :]
    gain = coef_ref[1:2, :]
    c2 = coef_ref[2:3, :]
    lagged = jnp.zeros_like(c0)
    rows = []
    for t in range(days):
        if t > 0:
            lagged = inflow[t - 1 : t, :] + c2 * lagged
        rows.append(c0 * inflow[t : t + 1, :] + gain * lagged)
    discharge = jnp.concatenate(rows, axis=0)
    out_ref[...] = discharge

    @pl.when(o < n_order - 1)
    def _():
        packed_val = None
        for part in split3(discharge):
            term = lax.dot_general(send_ref[...], part, (((1,), (1,)), ((), ())),
                                   preferred_element_type=jnp.float32)
            packed_val = term if packed_val is None else packed_val + term
        packed[...] = packed_val

        def start(j, carry):
            pltpu.make_async_remote_copy(
                src_ref=packed.at[pl.ds(j * cap, cap)],
                dst_ref=recv.at[pl.ds(b * cap, cap)],
                send_sem=send_sem.at[j],
                recv_sem=recv_sem.at[b],
                device_id=(o + 1, j),
                device_id_type=MESH,
            ).start()
            return carry
        lax.fori_loop(0, n_basin, start, 0)

        def finish(j, carry):
            pltpu.make_async_remote_copy(
                src_ref=packed.at[pl.ds(j * cap, cap)],
                dst_ref=recv.at[pl.ds(b * cap, cap)],
                send_sem=send_sem.at[j],
                recv_sem=recv_sem.at[b],
                device_id=(o + 1, j),
                device_id_type=MESH,
            ).wait_send()
            return carry
        lax.fori_loop(0, n_basin, finish, 0)


def route_chain(runoff, coef, send_t, table, n_order, n_basin, cap):
    days, reaches = runoff.shape
    slots = n_basin * cap
    vmem = pl.BlockSpec(memory_space=pltpu.VMEM)
    return pl.pallas_call(
        functools.partial(chain_kernel, n_order, n_basin, cap),
        out_shape=jax.ShapeDtypeStruct((days, reaches), jnp.float32),
        in_specs=[vmem] * 4,
        out_specs=vmem,
        scratch_shapes=[
            pltpu.VMEM((slots, days), jnp.float32),
            pltpu.VMEM((slots, days), jnp.float32),
            pltpu.SemaphoreType.DMA((n_basin,)),
            pltpu.SemaphoreType.DMA((n_basin,)),
        ],
        compiler_params=pltpu.CompilerParams(collective_id=0, has_side_effects=True),
    )(runoff, coef, send_t, table)


def per_device(
    forcings, w_input, w_recur, gate_bias, w_runoff, travel_time, weight_x, drain_basin, drain_reach
):
    basins = lax.axis_size("basin")
    groups = lax.axis_size("order")
    day_count = forcings.shape[0]
    reach_count = forcings.shape[2]
    units = w_recur.shape[1]
    capacity = 2 * reach_count // basins
    slots = basins * capacity
    drain_to = drain_basin[:, 0]
    onehot_drain = (drain_to[:, None] == jnp.arange(basins, dtype=jnp.int32)[None, :]).astype(
        jnp.int32
    )
    slot_index = jnp.sum(jnp.cumsum(onehot_drain, axis=0) * onehot_drain, axis=1) - 1
    flat_slot = drain_to * capacity + slot_index
    send_int = (
        flat_slot[:, None] == jnp.arange(slots, dtype=jnp.int32)[None, :]
    ).astype(jnp.int32)
    sent_targets = (jnp.dot(drain_reach[:, 0] + 1, send_int) - 1).reshape(basins, capacity)
    gathered = lax.all_to_all(sent_targets, "basin", split_axis=0, concat_axis=0, tiled=True)
    targets = lax.ppermute(gathered, "order", [(i, i + 1) for i in range(groups - 1)])
    table = (
        targets.reshape(-1)[:, None] == jnp.arange(reach_count, dtype=jnp.int32)[None, :]
    ).astype(jnp.bfloat16)
    send_t = (
        jnp.arange(slots, dtype=jnp.int32)[:, None] == flat_slot[None, :]
    ).astype(jnp.bfloat16)

    denominator = travel_time * (1.0 - weight_x) + 0.5
    coeff_first = (0.5 - travel_time * weight_x) / denominator
    coeff_second = (0.5 + travel_time * weight_x) / denominator
    recession = (travel_time * (1.0 - weight_x) - 0.5) / denominator
    gain = coeff_first * recession + coeff_second
    coef = jnp.zeros((8, reach_count), jnp.float32)
    coef = coef.at[0].set(coeff_first).at[1].set(gain).at[2].set(recession)

    lstm_state = (
        jnp.zeros((units, reach_count), jnp.bfloat16),
        jnp.zeros((units, reach_count), jnp.float32),
    )
    _, runoff = lstm_days(lstm_state, forcings, w_input, w_recur, gate_bias, w_runoff)
    return route_chain(runoff, coef, send_t, table, groups, basins, capacity)


def solution(mesh):
    return jax.shard_map(
        per_device,
        mesh=mesh,
        in_specs=(
            P(None, None, ("order", "basin")),
            P(),
            P(),
            P(),
            P(),
            P(("order", "basin")),
            P(("order", "basin")),
            P(("order", "basin"), None),
            P(("order", "basin"), None),
        ),
        out_specs=P(None, ("order", "basin")),
        check_vma=False,
    )
```

profile of v0, /device:TPU:89, one launch (start us, length us, event | category | flops | bytes accessed | tf_op | source)
XLA Modules:
  0.0 195.3 jit_solution(14807633867754435708)
XLA Ops:
  0.7 1.2 reduce-window.6
  4.3 1.6 fusion.26
  6.6 10.2 %all-to-all-start = ((s32[32,1,32]{2,1,0:T(1,128)}), s32[32,1,32]{2,1,0:T(1,128)S(1)}, u32[]{:S(2)}, u32[]{:S(2)}) async-start(s32[32,1,32]{2,1,0:T(1,128)} %all_to_all.8), calls=%async_computation | async-start | bytes 32768 | tf_op jit(solution)/shard_map/all_to_all | solution.py:185
  16.8 77.9 %while.18 = (s32[]{:T(128)}, bf16[128,512]{0,1:T(8,128)(2,1)S(1)}, f32[128,512]{0,1:T(8,128)S(1)}, f32[32,512]{1,0:T(8,128)S(1)}, bf16[32,16,512]{2,1,0:T(8,128)...) while((s32[]{:T(128)}, bf16[128,512]{0,1:T(8,128)(2,1)S(1)}, ...), condition=%wide.region_1.2_spmd.clone, body=%wide.region_0.0_spmd.clone.sunk | while | flops 77859840 | bytes 5823196 | solution.py:34
  16.9 1.1 convolution_bitcast_fusion.2
  19.3 1.1 convolution_bitcast_fusion.2
  21.7 1.1 convolution_bitcast_fusion.2
  24.2 1.1 convolution_bitcast_fusion.2
  31.5 1.1 convolution_bitcast_fusion.2
  33.9 1.1 convolution_bitcast_fusion.2
  43.6 1.1 convolution_bitcast_fusion.2
  46.1 1.1 convolution_bitcast_fusion.2
  53.4 1.1 convolution_bitcast_fusion.2
  55.8 1.1 convolution_bitcast_fusion.2
  58.2 1.1 convolution_bitcast_fusion.2
  65.5 1.1 convolution_bitcast_fusion.2
  68.0 1.1 convolution_bitcast_fusion.2
  70.4 1.1 convolution_bitcast_fusion.2
  94.7 1.4 fusion.24.send_ref
  96.1 1.3 collective-permute-start
  97.6 2.3 %collective-permute-done = s32[32,32]{1,0:T(8,128)S(1)} collective-permute-done((s32[32,32]{1,0:T(8,128)S(1)}, s32[32,32]{1,0:T(8,128)S(1)}, u32[]{:S(2)}, u32[]{:S(2)}) %collective-permute-start) | collective-permute-done | bytes 4128 | tf_op jit(solution)/shard_map/ppermute | solution.py:186
  100.0 1.3 fusion.25.table_ref
  101.3 92.6 %shard_map.91 = f32[32,512]{1,0:T(8,128)} custom-call(f32[32,512]{1,0:T(8,128)S(1)} %get-tuple-element.88.runoff_ref, f32[8,512]{1,0:T(8,128)} %copy-done.1, bf16[1024,512]{1,0:T(8,128)(2,1)} %fusion.24.send_ref, bf16[1024,512]{1,0:T(8,128)(2,1)} %fusion.25.table_ref), custom_call_target="tpu_custom_call" | custom-call | tf_op jit(solution)/shard_map/pallas_call | solution.py:150
  193.9 1.5 copy.32
  (394 shorter events, 63.6 us)
Async XLA Ops:
  6.6 89.5 %all-to-all-start = ((s32[32,1,32]{2,1,0:T(1,128)}), s32[32,1,32]{2,1,0:T(1,128)S(1)}, u32[]{:S(2)}, u32[]{:S(2)}) async-start(s32[32,1,32]{2,1,0:T(1,128)} %all_to_all.8), calls=%async_computation | async-start | bytes 32768 | tf_op jit(solution)/shard_map/all_to_all | solution.py:185
  16.8 1.1 copy-start
  19.3 1.1 copy-start
  21.7 1.1 copy-start
  26.6 1.1 copy-start
  29.0 1.1 copy-start
  31.4 1.1 copy-start
  36.3 1.1 copy-start
  38.7 1.1 copy-start
  41.2 1.1 copy-start
  43.6 1.1 copy-start
  48.5 1.1 copy-start
  50.9 1.1 copy-start
  53.4 1.1 copy-start
  55.8 1.1 copy-start
  60.7 1.1 copy-start
  63.1 1.1 copy-start
  65.5 1.1 copy-start
  68.0 1.1 copy-start
  72.8 1.1 copy-start
  94.7 2.7 %copy-start.4 = (f32[512]{0:T(512)S(1)}, f32[512]{0:T(512)}, u32[]{:S(2)}) copy-start(f32[512]{0:T(512)} %param.22) | copy-start | bytes 6148
  94.7 2.7 %copy-start.5 = (f32[512]{0:T(512)S(1)}, f32[512]{0:T(512)}, u32[]{:S(2)}) copy-start(f32[512]{0:T(512)} %param.23) | copy-start | bytes 6148
  96.1 3.8 %collective-permute-start = (s32[32,32]{1,0:T(8,128)S(1)}, s32[32,32]{1,0:T(8,128)S(1)}, u32[]{:S(2)}, u32[]{:S(2)}) collective-permute-start(s32[32,32]{1,0:T(8,128)S(1)} %bitcast.59), channel_id=1, source_target_pairs={{0,32},{32,64},{64,96},{96,128},{128,160},{160,192},{192,224},{1,3... | collective-permute-start | bytes 12296 | tf_op jit(solution)/shard_map/ppermute | solution.py:186
  97.6 3.7 %copy-start.1 = (f32[8,512]{1,0:T(8,128)}, f32[8,512]{1,0:T(8,128)S(1)}, u32[]{:S(2)}) copy-start(f32[8,512]{1,0:T(8,128)S(1)} %scatter.14.coef_ref) | copy-start | bytes 49156
  (77 other events, 72.1 us)
where the time goes:
time: 199 us; the launch traced here: 195 us
  Pallas kernels  92.6 us (47%)
  matrix products  52.8 us (27%)
  other arithmetic  16.7 us (8%)
  local copies, waits for them, and re-layouts  16.4 us (8%)
  starting transfers between devices  11.5 us (6%)
  loops' own time  2.9 us (1%)
  waiting for transfers between devices  2.32 us (1%)
    pallas_call x1, Pallas kernels, route_chain(): pl.pallas_call(functools.partial(chain_kernel, n_order, n_basin, cap), ou...  92.6 us
    dot_general x32, matrix products, one_day(): jnp.dot(w_input, inputs, preferred_element_type=jnp.float32)  35.3 us
    while x192, local copies, waits for them, and re-layouts  11.8 us
    all_to_all x1, starting transfers between devices, per_device(): lax.all_to_all(sent_targets, 'basin', split_axis=0, concat_axis=0, tiled=...  10.2 us
    dot_general x32, matrix products, one_day(): jnp.dot(w_recur, hidden, preferred_element_type=jnp.float32)  9.55 us
    convert_element_type x32, other arithmetic, one_day(): hidden = (outgate * jnp.tanh(memory)).astype(jnp.bfloat16)  9.23 us
    dot_general x32, matrix products, one_day(): jnp.dot(w_runoff, hidden.astype(jnp.float32), precision=lax.Precision.HIG...  6.3 us
  transfers between devices with their start and end apart: 2, of which 1 were waited for; matrix products, arithmetic and copies ran while one was open for 33% of the time, Pallas kernels for 0%

commit v1 on v0

--- a/solution.py
+++ b/solution.py
@@ -34,12 +34,10 @@
     return lax.scan(one_day, lstm_state, day_block)
 
 
-def split3(x):
+def split2(x):
     hi = x.astype(jnp.bfloat16)
-    rest = x - hi.astype(jnp.float32)
-    mid = rest.astype(jnp.bfloat16)
-    lo = (rest - mid.astype(jnp.float32)).astype(jnp.bfloat16)
-    return hi, mid, lo
+    lo = (x - hi.astype(jnp.float32)).astype(jnp.bfloat16)
+    return hi, lo
 
 
 def chain_kernel(n_order, n_basin, cap, runoff_ref, coef_ref, send_ref, table_ref, out_ref,
@@ -90,7 +88,7 @@
             return carry
         lax.fori_loop(0, n_basin, arrived, 0)
         arrive = None
-        for part in split3(recv[...]):
+        for part in split2(recv[...]):
             term = lax.dot_general(part, table_ref[...], (((0,), (0,)), ((), ())),
                                    preferred_element_type=jnp.float32)
             arrive = term if arrive is None else arrive + term
@@ -112,7 +110,7 @@
     @pl.when(o < n_order - 1)
     def _():
         packed_val = None
-        for part in split3(discharge):
+        for part in split2(discharge):
             term = lax.dot_general(send_ref[...], part, (((1,), (1,)), ((), ())),
                                    preferred_element_type=jnp.float32)
             packed_val = term if packed_val is None else packed_val + term

time: 199 us -> 196 us (0.985)
  Pallas kernels: 92.6 us -> 89.4 us
    pallas_call x1, Pallas kernels: 92.6 us -> 89.4 us  [route_chain(): pl.pallas_call(functools.partial(chain_kernel, n_order, n_basin, cap), ou...]
  transfers between devices with their start and end apart: 2 -> 2, of which waited for: 1 -> 1; matrix products, arithmetic and copies ran while one was open for 33% -> 34% of each run, Pallas kernels for 0% -> 0%
where the time goes in v1:
time: 196 us; the launch traced here: 192 us
  Pallas kernels  89.4 us (46%)
  matrix products  52.8 us (27%)
  other arithmetic  16.7 us (9%)
  local copies, waits for them, and re-layouts  16.4 us (8%)
  starting transfers between devices  11.5 us (6%)
  loops' own time  2.9 us (1%)
  waiting for transfers between devices  2.32 us (1%)
    pallas_call x1, Pallas kernels, route_chain(): pl.pallas_call(functools.partial(chain_kernel, n_order, n_basin, cap), ou...  89.4 us
    dot_general x32, matrix products, one_day(): jnp.dot(w_input, inputs, preferred_element_type=jnp.float32)  35.3 us
    while x192, local copies, waits for them, and re-layouts  11.8 us
    all_to_all x1, starting transfers between devices, per_device(): lax.all_to_all(sent_targets, 'basin', split_axis=0, concat_axis=0, tiled=...  10.2 us
    dot_general x32, matrix products, one_day(): jnp.dot(w_recur, hidden, preferred_element_type=jnp.float32)  9.55 us
    convert_element_type x32, other arithmetic, one_day(): hidden = (outgate * jnp.tanh(memory)).astype(jnp.bfloat16)  9.23 us
    dot_general x32, matrix products, one_day(): jnp.dot(w_runoff, hidden.astype(jnp.float32), precision=lax.Precision.HIG...  6.3 us
  transfers between devices with their start and end apart: 2, of which 1 were waited for; matrix products, arithmetic and copies ran while one was open for 34% of the time, Pallas kernels for 0%

profile of v1, /device:TPU:89, one launch (start us, length us, event | category | flops | bytes accessed | tf_op | source)
XLA Modules:
  0.0 192.1 jit_solution(9938416862347014538)
XLA Ops:
  0.7 1.2 reduce-window.6
  4.3 1.6 fusion.26
  6.6 10.2 %all-to-all-start = ((s32[32,1,32]{2,1,0:T(1,128)}), s32[32,1,32]{2,1,0:T(1,128)S(1)}, u32[]{:S(2)}, u32[]{:S(2)}) async-start(s32[32,1,32]{2,1,0:T(1,128)} %all_to_all.8), calls=%async_computation | async-start | bytes 32768 | tf_op jit(solution)/shard_map/all_to_all | solution.py:183
  16.8 77.9 %while.18 = (s32[]{:T(128)}, bf16[128,512]{0,1:T(8,128)(2,1)S(1)}, f32[128,512]{0,1:T(8,128)S(1)}, f32[32,512]{1,0:T(8,128)S(1)}, bf16[32,16,512]{2,1,0:T(8,128)...) while((s32[]{:T(128)}, bf16[128,512]{0,1:T(8,128)(2,1)S(1)}, ...), condition=%wide.region_1.2_spmd.clone, body=%wide.region_0.0_spmd.clone.sunk | while | flops 77859840 | bytes 5823196 | solution.py:34
  16.9 1.1 convolution_bitcast_fusion.2
  19.3 1.1 convolution_bitcast_fusion.2
  21.7 1.1 convolution_bitcast_fusion.2
  24.2 1.1 convolution_bitcast_fusion.2
  31.5 1.1 convolution_bitcast_fusion.2
  33.9 1.1 convolution_bitcast_fusion.2
  43.6 1.1 convolution_bitcast_fusion.2
  46.1 1.1 convolution_bitcast_fusion.2
  53.4 1.1 convolution_bitcast_fusion.2
  55.8 1.1 convolution_bitcast_fusion.2
  58.2 1.1 convolution_bitcast_fusion.2
  65.5 1.1 convolution_bitcast_fusion.2
  68.0 1.1 convolution_bitcast_fusion.2
  70.4 1.1 convolution_bitcast_fusion.2
  94.7 1.4 fusion.24.send_ref
  96.1 1.3 collective-permute-start
  97.6 2.3 %collective-permute-done = s32[32,32]{1,0:T(8,128)S(1)} collective-permute-done((s32[32,32]{1,0:T(8,128)S(1)}, s32[32,32]{1,0:T(8,128)S(1)}, u32[]{:S(2)}, u32[]{:S(2)}) %collective-permute-start) | collective-permute-done | bytes 4128 | tf_op jit(solution)/shard_map/ppermute | solution.py:184
  100.0 1.3 fusion.25.table_ref
  101.3 89.4 %shard_map.91 = f32[32,512]{1,0:T(8,128)} custom-call(f32[32,512]{1,0:T(8,128)S(1)} %get-tuple-element.88.runoff_ref, f32[8,512]{1,0:T(8,128)} %copy-done.1, bf16[1024,512]{1,0:T(8,128)(2,1)} %fusion.24.send_ref, bf16[1024,512]{1,0:T(8,128)(2,1)} %fusion.25.table_ref), custom_call_target="tpu_custom_call" | custom-call | tf_op jit(solution)/shard_map/pallas_call | solution.py:148
  190.7 1.5 copy.32
  (394 shorter events, 63.6 us)
Async XLA Ops:
  6.6 89.5 %all-to-all-start = ((s32[32,1,32]{2,1,0:T(1,128)}), s32[32,1,32]{2,1,0:T(1,128)S(1)}, u32[]{:S(2)}, u32[]{:S(2)}) async-start(s32[32,1,32]{2,1,0:T(1,128)} %all_to_all.8), calls=%async_computation | async-start | bytes 32768 | tf_op jit(solution)/shard_map/all_to_all | solution.py:183
  16.8 1.1 copy-start
  19.3 1.1 copy-start
  21.7 1.1 copy-start
  26.6 1.1 copy-start
  29.0 1.1 copy-start
  31.4 1.1 copy-start
  36.3 1.1 copy-start
  38.7 1.1 copy-start
  41.2 1.1 copy-start
  43.6 1.1 copy-start
  48.5 1.1 copy-start
  50.9 1.1 copy-start
  53.4 1.1 copy-start
  55.8 1.1 copy-start
  60.7 1.1 copy-start
  63.1 1.1 copy-start
  65.5 1.1 copy-start
  68.0 1.1 copy-start
  72.8 1.1 copy-start
  94.7 2.7 %copy-start.4 = (f32[512]{0:T(512)S(1)}, f32[512]{0:T(512)}, u32[]{:S(2)}) copy-start(f32[512]{0:T(512)} %param.22) | copy-start | bytes 6148
  94.7 2.7 %copy-start.5 = (f32[512]{0:T(512)S(1)}, f32[512]{0:T(512)}, u32[]{:S(2)}) copy-start(f32[512]{0:T(512)} %param.23) | copy-start | bytes 6148
  96.1 3.8 %collective-permute-start = (s32[32,32]{1,0:T(8,128)S(1)}, s32[32,32]{1,0:T(8,128)S(1)}, u32[]{:S(2)}, u32[]{:S(2)}) collective-permute-start(s32[32,32]{1,0:T(8,128)S(1)} %bitcast.59), channel_id=1, source_target_pairs={{0,32},{32,64},{64,96},{96,128},{128,160},{160,192},{192,224},{1,3... | collective-permute-start | bytes 12296 | tf_op jit(solution)/shard_map/ppermute | solution.py:184
  97.6 3.7 %copy-start.1 = (f32[8,512]{1,0:T(8,128)}, f32[8,512]{1,0:T(8,128)S(1)}, u32[]{:S(2)}) copy-start(f32[8,512]{1,0:T(8,128)S(1)} %scatter.14.coef_ref) | copy-start | bytes 49156
  (77 other events, 72.1 us)

commit v2 on v1

--- a/solution.py
+++ b/solution.py
@@ -32,6 +32,52 @@
         return ((hidden, memory), runoff)
 
     return lax.scan(one_day, lstm_state, day_block)
+
+
+def lstm_kernel(block, forc_ref, w_in_ref, w_rec_ref, bias_ref, w_ro_ref, out_ref, h_scr, c_scr):
+    days = forc_ref.shape[0]
+    units = w_rec_ref.shape[1]
+    reaches = out_ref.shape[2]
+    h_scr[...] = jnp.zeros_like(h_scr)
+    c_scr[...] = jnp.zeros_like(c_scr)
+
+    def day(t, carry):
+        for j in range(reaches // block):
+            cols = pl.ds(j * block, block)
+            gates = (
+                jnp.dot(w_in_ref[...], forc_ref[t, :, cols], preferred_element_type=jnp.float32)
+                + jnp.dot(w_rec_ref[...], h_scr[:, cols], preferred_element_type=jnp.float32)
+                + bias_ref[...]
+            )
+            ingate = jax.nn.sigmoid(gates[:units])
+            forget = jax.nn.sigmoid(gates[units : 2 * units])
+            candidate = jnp.tanh(gates[2 * units : 3 * units])
+            outgate = jax.nn.sigmoid(gates[3 * units :])
+            memory = forget * c_scr[:, cols] + ingate * candidate
+            hidden = (outgate * jnp.tanh(memory)).astype(jnp.bfloat16)
+            c_scr[:, cols] = memory
+            h_scr[:, cols] = hidden
+            z = jnp.sum(w_ro_ref[...] * hidden.astype(jnp.float32), axis=0, keepdims=True)
+            out_ref[t, :, cols] = jnp.maximum(z, 0.0) + jnp.log1p(jnp.exp(-jnp.abs(z)))
+        return carry
+
+    lax.fori_loop(0, days, day, 0)
+
+
+def lstm_runoff(forcings, w_input, w_recur, gate_bias, w_runoff, block=128):
+    days, _, reaches = forcings.shape
+    units = w_recur.shape[1]
+    vmem = pl.BlockSpec(memory_space=pltpu.VMEM)
+    return pl.pallas_call(
+        functools.partial(lstm_kernel, block),
+        out_shape=jax.ShapeDtypeStruct((days, 1, reaches), jnp.float32),
+        in_specs=[vmem] * 5,
+        out_specs=vmem,
+        scratch_shapes=[
+            pltpu.VMEM((units, reaches), jnp.bfloat16),
+            pltpu.VMEM((units, reaches), jnp.float32),
+        ],
+    )(forcings, w_input, w_recur, gate_bias[:, None], w_runoff[:, None]).reshape(days, reaches)
 
 
 def split2(x):
@@ -197,11 +243,7 @@
     coef = jnp.zeros((8, reach_count), jnp.float32)
     coef = coef.at[0].set(coeff_first).at[1].set(gain).at[2].set(recession)
 
-    lstm_state = (
-        jnp.zeros((units, reach_count), jnp.bfloat16),
-        jnp.zeros((units, reach_count), jnp.float32),
-    )
-    _, runoff = lstm_days(lstm_state, forcings, w_input, w_recur, gate_bias, w_runoff)
+    runoff = lstm_runoff(forcings, w_input, w_recur, gate_bias, w_runoff)
     return route_chain(runoff, coef, send_t, table, groups, basins, capacity)
 
 

time: 196 us -> 141 us (0.72)
  the two profiles are of different devices: /device:TPU:89 before, /device:TPU:25 now
where the time goes in v2:
time: 141 us; the launch traced here: 140 us
  Pallas kernels  106 us (75%)
  starting transfers between devices  12.3 us (9%)
  waiting for transfers between devices  7.1 us (5%)
  other arithmetic  6.79 us (5%)
  local copies, waits for them, and re-layouts  6.44 us (5%)
  matrix products  1.63 us (1%)
    pallas_call x1, Pallas kernels, route_chain(): pl.pallas_call(functools.partial(chain_kernel, n_order, n_basin, cap), ou...  87.3 us
    pallas_call x1, Pallas kernels, lstm_runoff(): pl.pallas_call(functools.partial(lstm_kernel, block), out_shape=jax.Shape...  18.7 us
    all_to_all x1, starting transfers between devices, per_device(): lax.all_to_all(sent_targets, 'basin', split_axis=0, concat_axis=0, tiled=...  11 us
    all_to_all x1, waiting for transfers between devices, per_device(): lax.all_to_all(sent_targets, 'basin', split_axis=0, concat_axis=0, tiled=...  7.1 us
    unnamed x15, local copies, waits for them, and re-layouts  3.72 us
  transfers between devices with their start and end apart: 2, of which 1 were waited for; matrix products, arithmetic and copies ran while one was open for 4% of the time, Pallas kernels for 13%

profile of v2, /device:TPU:25, one launch (start us, length us, event | category | flops | bytes accessed | tf_op | source)
XLA Modules:
  0.0 140.4 jit_solution(8734614048805411691)
XLA Ops:
  0.0 0.7 fusion.6
  0.8 1.2 reduce-window.6
  1.9 0.2 slice_reduce_fusion
  2.2 0.8 fusion.5
  3.0 0.7 broadcast_add_fusion.1
  3.7 0.7 multiply_add_fusion
  4.3 1.6 %fusion.2 = s32[1,1024]{1,0:T(1,128)S(1)} fusion(s32[512]{0:T(512)S(1)} %bitcast.41, s32[512,1]{0,1:T(1,128)} %param.23), kind=kOutput, calls=%fused_computation.5 | convolution fusion | flops 1573376 | bytes 8192 | tf_op jit(solution)/shard_map/dot_general | solution.py:228
  6.0 0.7 all_to_all.8
  6.7 11.0 %all-to-all-start = ((s32[32,1,32]{2,1,0:T(1,128)}), s32[32,1,32]{2,1,0:T(1,128)S(1)}, u32[]{:S(2)}, u32[]{:S(2)}) async-start(s32[32,1,32]{2,1,0:T(1,128)} %all_to_all.8), calls=%async_computation | async-start | bytes 32768 | tf_op jit(solution)/shard_map/all_to_all | solution.py:229
  17.7 1.4 %fusion.send_ref = bf16[1024,512]{1,0:T(8,128)(2,1)} fusion(s32[512]{0:T(512)S(1)} %get-tuple-element.45), kind=kLoop, calls=%fused_computation.3 | loop fusion | flops 1048576 | bytes 1050624 | tf_op jit(solution)/shard_map/convert_element_type | solution.py:236
  19.1 7.1 %all-to-all-done = s32[32,1,32]{2,1,0:T(1,128)S(1)} async-done(((s32[32,1,32]{2,1,0:T(1,128)}), s32[32,1,32]{2,1,0:T(1,128)S(1)}, u32[]{:S(2)}, u32[]{:S(2)}) %all-to-all-start) | async-done | bytes 4128 | tf_op jit(solution)/shard_map/all_to_all | solution.py:229
  26.2 1.3 collective-permute-start
  27.6 0.7 copy.14.w_ro_ref
  28.3 0.7 copy.12.w_in_ref
  29.1 0.0 copy-done.2
  29.1 0.9 copy.13.bias_ref
  29.9 18.7 %shard_map.91 = f32[32,1,512]{2,1,0:T(1,128)} custom-call(bf16[32,16,512]{2,1,0:T(8,128)(2,1)} %forc_ref.1, bf16[512,16]{1,0:T(8,128)(2,1)} %copy.12.w_in_ref, bf16[512,128]{1,0:T(8,128)(2,1)} %w_rec_ref.1, f32[512,1]{1,0:T(8,128)} %copy.13.bias_ref, f32[128,1]{1,0:T(8,128)} %copy.14.w_ro_ref), custom_call_target="tpu_custom_call" | custom-call | tf_op jit(solution)/shard_map/pallas_call | solution.py:71
  48.6 1.5 %copy.20 = f32[32,1,512]{2,0,1:T(8,128)} copy(f32[32,1,512]{2,1,0:T(1,128)} %shard_map.91) | data formatting | bytes 131072
  50.2 0.1 scatter.14.coef_ref
  50.2 0.0 collective-permute-done
  50.2 0.1 eq.80
  50.3 1.3 fusion.1.table_ref
  51.6 87.3 %shard_map.92 = f32[32,512]{1,0:T(8,128)} custom-call(f32[32,512]{1,0:T(8,128)} %bitcast.30, f32[8,512]{1,0:T(8,128)} %copy-done, bf16[1024,512]{1,0:T(8,128)(2,1)} %fusion.send_ref, bf16[1024,512]{1,0:T(8,128)(2,1)} %fusion.1.table_ref), custom_call_target="tpu_custom_call" | custom-call | tf_op jit(solution)/shard_map/pallas_call | solution.py:194
  138.9 1.5 %copy.24 = f32[32,512]{1,0:T(8,128)} copy(f32[32,512]{1,0:T(8,128)} %shard_map.92) | data formatting | bytes 131072
  (17 shorter events, 0.1 us)
Async XLA Ops:
  0.0 27.5 %copy-start.4 = (f32[512]{0:T(512)S(1)}, f32[512]{0:T(512)}, u32[]{:S(2)}) copy-start(f32[512]{0:T(512)} %param.21) | copy-start | bytes 6148
  0.0 27.5 %copy-start.3 = (f32[512]{0:T(512)S(1)}, f32[512]{0:T(512)}, u32[]{:S(2)}) copy-start(f32[512]{0:T(512)} %param.20) | copy-start | bytes 6148
  0.0 27.6 %copy-start.5 = (f32[128]{0:T(128)S(1)}, f32[128]{0:T(128)}, u32[]{:S(2)}) copy-start(f32[128]{0:T(128)} %param.19) | copy-start | bytes 1540
  0.0 28.3 %copy-start.1 = (bf16[512,16]{0,1:T(8,128)(2,1)S(1)}, bf16[512,16]{0,1:T(8,128)(2,1)}, u32[]{:S(2)}) copy-start(bf16[512,16]{0,1:T(8,128)(2,1)} %param.16) | copy-start | bytes 49156
  1.9 27.2 %copy-start.2 = (f32[512]{0:T(512)S(1)}, f32[512]{0:T(512)}, u32[]{:S(2)}) copy-start(f32[512]{0:T(512)} %param.18) | copy-start | bytes 6148
  6.7 19.5 %all-to-all-start = ((s32[32,1,32]{2,1,0:T(1,128)}), s32[32,1,32]{2,1,0:T(1,128)S(1)}, u32[]{:S(2)}, u32[]{:S(2)}) async-start(s32[32,1,32]{2,1,0:T(1,128)} %all_to_all.8), calls=%async_computation | async-start | bytes 32768 | tf_op jit(solution)/shard_map/all_to_all | solution.py:229
  26.2 24.0 %collective-permute-start = (s32[32,32]{1,0:T(8,128)S(1)}, s32[32,32]{1,0:T(8,128)S(1)}, u32[]{:S(2)}, u32[]{:S(2)}) collective-permute-start(s32[32,32]{1,0:T(8,128)S(1)} %bitcast.34), channel_id=1, source_target_pairs={{0,32},{32,64},{64,96},{96,128},{128,160},{160,192},{192,224},{1,3... | collective-permute-start | bytes 12296 | tf_op jit(solution)/shard_map/ppermute | solution.py:230
  50.2 1.4 copy-start

commit v3 on v2

--- a/solution.py
+++ b/solution.py
@@ -86,8 +86,8 @@
     return hi, lo
 
 
-def chain_kernel(n_order, n_basin, cap, runoff_ref, coef_ref, send_ref, table_ref, out_ref,
-                 packed, recv, send_sem, recv_sem):
+def chain_kernel(n_order, n_basin, cap, runoff_ref, coef_ref, send_ref, tgt_ref, out_ref,
+                 packed, recv, table_ref, tgt_recv, send_sem, recv_sem, tsend_sem, trecv_sem):
     o = lax.axis_index("order")
     b = lax.axis_index("basin")
     days = runoff_ref.shape[0]
@@ -118,10 +118,41 @@
     def _():
         pl.semaphore_wait(barrier, 2 * n_basin)
 
+    def target_copy(j, row):
+        return pltpu.make_async_remote_copy(
+            src_ref=tgt_ref.at[pl.ds(j * cap, cap)],
+            dst_ref=tgt_recv.at[pl.ds(row * cap, cap)],
+            send_sem=tsend_sem.at[j],
+            recv_sem=trecv_sem.at[row],
+            device_id=(o + 1, j),
+            device_id_type=MESH,
+        )
+
+    @pl.when(o < n_order - 1)
+    def _():
+        def start(j, carry):
+            target_copy(j, b).start()
+            return carry
+        lax.fori_loop(0, n_basin, start, 0)
+
     out_ref[...] = runoff_ref[...]
 
     @pl.when(o > 0)
     def _():
+        def got(j, carry):
+            pltpu.make_async_remote_copy(
+                src_ref=tgt_ref.at[pl.ds(j * cap, cap)],
+                dst_ref=tgt_recv.at[pl.ds(j * cap, cap)],
+                send_sem=tsend_sem.at[j],
+                recv_sem=trecv_sem.at[j],
+                device_id=(o - 1, j),
+                device_id_type=MESH,
+            ).wait_recv()
+            return carry
+        lax.fori_loop(0, n_basin, got, 0)
+        reach = lax.broadcasted_iota(jnp.int32, (1, table_ref.shape[1]), 1)
+        table_ref[...] = (tgt_recv[...] == reach).astype(jnp.bfloat16)
+
         def arrived(j, carry):
             pltpu.make_async_remote_copy(
                 src_ref=packed.at[pl.ds(j * cap, cap)],
@@ -186,8 +217,13 @@
             return carry
         lax.fori_loop(0, n_basin, finish, 0)
 
-
-def route_chain(runoff, coef, send_t, table, n_order, n_basin, cap):
+        def finish_targets(j, carry):
+            target_copy(j, b).wait_send()
+            return carry
+        lax.fori_loop(0, n_basin, finish_targets, 0)
+
+
+def route_chain(runoff, coef, send_t, tgt, n_order, n_basin, cap):
     days, reaches = runoff.shape
     slots = n_basin * cap
     vmem = pl.BlockSpec(memory_space=pltpu.VMEM)
@@ -199,11 +235,15 @@
         scratch_shapes=[
             pltpu.VMEM((slots, days), jnp.float32),
             pltpu.VMEM((slots, days), jnp.float32),
+            pltpu.VMEM((slots, reaches), jnp.bfloat16),
+            pltpu.VMEM((slots, 1), jnp.int32),
+            pltpu.SemaphoreType.DMA((n_basin,)),
+            pltpu.SemaphoreType.DMA((n_basin,)),
             pltpu.SemaphoreType.DMA((n_basin,)),
             pltpu.SemaphoreType.DMA((n_basin,)),
         ],
         compiler_params=pltpu.CompilerParams(collective_id=0, has_side_effects=True),
-    )(runoff, coef, send_t, table)
+    )(runoff, coef, send_t, tgt)
 
 
 def per_device(
@@ -225,12 +265,7 @@
     send_int = (
         flat_slot[:, None] == jnp.arange(slots, dtype=jnp.int32)[None, :]
     ).astype(jnp.int32)
-    sent_targets = (jnp.dot(drain_reach[:, 0] + 1, send_int) - 1).reshape(basins, capacity)
-    gathered = lax.all_to_all(sent_targets, "basin", split_axis=0, concat_axis=0, tiled=True)
-    targets = lax.ppermute(gathered, "order", [(i, i + 1) for i in range(groups - 1)])
-    table = (
-        targets.reshape(-1)[:, None] == jnp.arange(reach_count, dtype=jnp.int32)[None, :]
-    ).astype(jnp.bfloat16)
+    sent_targets = (jnp.dot(drain_reach[:, 0] + 1, send_int) - 1).reshape(slots, 1)
     send_t = (
         jnp.arange(slots, dtype=jnp.int32)[:, None] == flat_slot[None, :]
     ).astype(jnp.bfloat16)
@@ -244,7 +279,7 @@
     coef = coef.at[0].set(coeff_first).at[1].set(gain).at[2].set(recession)
 
     runoff = lstm_runoff(forcings, w_input, w_recur, gate_bias, w_runoff)
-    return route_chain(runoff, coef, send_t, table, groups, basins, capacity)
+    return route_chain(runoff, coef, send_t, sent_targets, groups, basins, capacity)
 
 
 def solution(mesh):

time: 141 us -> 135 us (0.957); the launches traced: 140 us -> 132 us
  starting transfers between devices: 12.3 us -> 0 us
  Pallas kernels: 106 us -> 117 us
  waiting for transfers between devices: 7.1 us -> 0 us
    pallas_call x1, Pallas kernels: 87.3 us -> 98.5 us  [route_chain(): pl.pallas_call(functools.partial(chain_kernel, n_order, n_basin, cap), ou...]
    all_to_all x1 -> x0, starting transfers between devices: 11 us -> none  [per_device(): lax.all_to_all(sent_targets, 'basin', split_axis=0, concat_axis=0, tiled=...]
    all_to_all x1 -> x0, waiting for transfers between devices: 7.1 us -> none  [per_device(): lax.all_to_all(sent_targets, 'basin', split_axis=0, concat_axis=0, tiled=...]
    unnamed x15 -> x9, local copies, waits for them, and re-layouts: 3.72 us -> 3.72 us
  transfers between devices with their start and end apart: 2 -> 0, of which waited for: 1 -> 0; matrix products, arithmetic and copies ran while one was open for 4% -> 0% of each run, Pallas kernels for 13% -> 0%
where the time goes in v3:
time: 135 us; the launch traced here: 132 us
  Pallas kernels  117 us (87%)
  local copies, waits for them, and re-layouts  7.36 us (5%)
  other arithmetic  6.19 us (5%)
  matrix products  1.63 us (1%)
    pallas_call x1, Pallas kernels, route_chain(): pl.pallas_call(functools.partial(chain_kernel, n_order, n_basin, cap), ou...  98.5 us
    pallas_call x1, Pallas kernels, lstm_runoff(): pl.pallas_call(functools.partial(lstm_kernel, block), out_shape=jax.Shape...  18.6 us
    unnamed x9, local copies, waits for them, and re-layouts  3.72 us

profile of v3, /device:TPU:25, one launch (start us, length us, event | category | flops | bytes accessed | tf_op | source)
XLA Modules:
  0.0 132.3 jit_solution(14642527804520077534)
XLA Ops:
  0.0 0.0 copy-start.2
  0.0 0.7 add_divide_fusion
  0.7 0.1 scatter.11
  0.8 0.1 scatter.14.coef_ref
  0.9 0.0 copy-start
  0.9 1.4 %copy.14.w_ro_ref = f32[128,1]{1,0:T(8,128)} copy(f32[128,1]{0,1:T(1,128)} %bitcast.42) | data formatting | bytes 1024 | tf_op jit(solution)/shard_map/broadcast_in_dim | solution.py:80
  2.3 0.7 fusion.5
  3.0 1.2 reduce-window.6
  4.1 0.2 slice_reduce_fusion
  4.4 0.8 fusion.4
  5.2 0.7 broadcast_add_fusion.1
  5.9 0.7 multiply_add_fusion
  6.5 1.6 %fusion.1 = s32[1,1024]{1,0:T(1,128)S(1)} fusion(s32[512]{0:T(512)S(1)} %bitcast.41, s32[512,1]{0,1:T(1,128)} %param.23), kind=kOutput, calls=%fused_computation.3 | convolution fusion | flops 1573376 | bytes 8192 | tf_op jit(solution)/shard_map/dot_general | solution.py:268
  8.2 0.0 copy-done.1
  8.2 0.8 copy.12.w_in_ref
  9.0 0.0 copy-done.2
  9.0 0.8 copy.13.bias_ref
  9.8 18.6 %shard_map.91 = f32[32,1,512]{2,1,0:T(1,128)} custom-call(bf16[32,16,512]{2,1,0:T(8,128)(2,1)} %forc_ref.1, bf16[512,16]{1,0:T(8,128)(2,1)} %copy.12.w_in_ref, bf16[512,128]{1,0:T(8,128)(2,1)} %w_rec_ref.1, f32[512,1]{1,0:T(8,128)} %copy.13.bias_ref, f32[128,1]{1,0:T(8,128)} %copy.14.w_ro_ref), custom_call_target="tpu_custom_call" | custom-call | tf_op jit(solution)/shard_map/pallas_call | solution.py:71
  28.4 0.0 copy-done
  28.4 1.5 %copy.21 = f32[32,1,512]{2,0,1:T(8,128)} copy(f32[32,1,512]{2,1,0:T(1,128)} %shard_map.91) | data formatting | bytes 131072
  29.9 1.0 copy.16.tgt_ref
  30.9 1.4 %fusion.send_ref = bf16[1024,512]{1,0:T(8,128)(2,1)} fusion(s32[512]{0:T(512)S(1)} %get-tuple-element.45), kind=kLoop, calls=%fused_computation.2 | loop fusion | flops 1048576 | bytes 1050624 | tf_op jit(solution)/shard_map/convert_element_type | solution.py:271
  32.3 98.5 %shard_map.92 = f32[32,512]{1,0:T(8,128)} custom-call(f32[32,512]{1,0:T(8,128)} %bitcast.30, f32[8,512]{1,0:T(8,128)} %copy-done, bf16[1024,512]{1,0:T(8,128)(2,1)} %fusion.send_ref, s32[1024,1]{1,0:T(8,128)} %copy.16.tgt_ref), custom_call_target="tpu_custom_call" | custom-call | tf_op jit(solution)/shard_map/pallas_call | solution.py:230
  130.9 1.5 %copy.25 = f32[32,512]{1,0:T(8,128)} copy(f32[32,512]{1,0:T(8,128)} %shard_map.92) | data formatting | bytes 131072
  (5 shorter events, 0.1 us)
Async XLA Ops:
  0.0 9.0 %copy-start.2 = (f32[512]{0:T(512)S(1)}, f32[512]{0:T(512)}, u32[]{:S(2)}) copy-start(f32[512]{0:T(512)} %param.18) | copy-start | bytes 6148
  0.0 8.2 %copy-start.1 = (bf16[512,16]{0,1:T(8,128)(2,1)S(1)}, bf16[512,16]{0,1:T(8,128)(2,1)}, u32[]{:S(2)}) copy-start(bf16[512,16]{0,1:T(8,128)(2,1)} %param.16) | copy-start | bytes 49156
  0.9 27.5 %copy-start = (f32[8,512]{1,0:T(8,128)}, f32[8,512]{1,0:T(8,128)S(1)}, u32[]{:S(2)}) copy-start(f32[8,512]{1,0:T(8,128)S(1)} %scatter.14.coef_ref) | copy-start | bytes 49156

commit v4 on v3

--- a/solution.py
+++ b/solution.py
@@ -87,10 +87,12 @@
 
 
 def chain_kernel(n_order, n_basin, cap, runoff_ref, coef_ref, send_ref, tgt_ref, out_ref,
-                 packed, recv, table_ref, tgt_recv, send_sem, recv_sem, tsend_sem, trecv_sem):
+                 packed, recv, table_ref, tgt_recv, spread, send_sem, recv_sem, tsend_sem, trecv_sem):
     o = lax.axis_index("order")
     b = lax.axis_index("basin")
-    days = runoff_ref.shape[0]
+    days, reaches = runoff_ref.shape
+    groups = cap // 8
+    rows = 8
 
     barrier = pltpu.get_barrier_semaphore()
 
@@ -118,57 +120,60 @@
     def _():
         pl.semaphore_wait(barrier, 2 * n_basin)
 
-    def target_copy(j, row):
+    def target_copy(j, row, peer):
         return pltpu.make_async_remote_copy(
-            src_ref=tgt_ref.at[pl.ds(j * cap, cap)],
-            dst_ref=tgt_recv.at[pl.ds(row * cap, cap)],
+            src_ref=tgt_ref.at[pl.ds(j * rows, rows)],
+            dst_ref=tgt_recv.at[pl.ds(row * rows, rows)],
             send_sem=tsend_sem.at[j],
             recv_sem=trecv_sem.at[row],
-            device_id=(o + 1, j),
+            device_id=(peer, j),
             device_id_type=MESH,
         )
 
+    def data_copy(j, row, peer):
+        return pltpu.make_async_remote_copy(
+            src_ref=packed.at[pl.ds(j * rows, rows)],
+            dst_ref=recv.at[pl.ds(row * rows, rows)],
+            send_sem=send_sem.at[j],
+            recv_sem=recv_sem.at[row],
+            device_id=(peer, j),
+            device_id_type=MESH,
+        )
+
     @pl.when(o < n_order - 1)
     def _():
         def start(j, carry):
-            target_copy(j, b).start()
+            target_copy(j, b, o + 1).start()
             return carry
         lax.fori_loop(0, n_basin, start, 0)
 
+    spread[...] = jnp.zeros_like(spread)
     out_ref[...] = runoff_ref[...]
 
     @pl.when(o > 0)
     def _():
         def got(j, carry):
-            pltpu.make_async_remote_copy(
-                src_ref=tgt_ref.at[pl.ds(j * cap, cap)],
-                dst_ref=tgt_recv.at[pl.ds(j * cap, cap)],
-                send_sem=tsend_sem.at[j],
-                recv_sem=trecv_sem.at[j],
-                device_id=(o - 1, j),
-                device_id_type=MESH,
-            ).wait_recv()
+            target_copy(j, j, o - 1).wait_recv()
             return carry
         lax.fori_loop(0, n_basin, got, 0)
-        reach = lax.broadcasted_iota(jnp.int32, (1, table_ref.shape[1]), 1)
-        table_ref[...] = (tgt_recv[...] == reach).astype(jnp.bfloat16)
+        reach = lax.broadcasted_iota(jnp.int32, (1, reaches), 1)
+        for k in range(groups):
+            table_ref[:, k * reaches : (k + 1) * reaches] = (
+                tgt_recv[:, k : k + 1] == reach
+            ).astype(jnp.bfloat16)
 
         def arrived(j, carry):
-            pltpu.make_async_remote_copy(
-                src_ref=packed.at[pl.ds(j * cap, cap)],
-                dst_ref=recv.at[pl.ds(j * cap, cap)],
-                send_sem=send_sem.at[j],
-                recv_sem=recv_sem.at[j],
-                device_id=(o - 1, j),
-                device_id_type=MESH,
-            ).wait_recv()
+            data_copy(j, j, o - 1).wait_recv()
             return carry
         lax.fori_loop(0, n_basin, arrived, 0)
-        arrive = None
+        wide = None
         for part in split2(recv[...]):
             term = lax.dot_general(part, table_ref[...], (((0,), (0,)), ((), ())),
                                    preferred_element_type=jnp.float32)
-            arrive = term if arrive is None else arrive + term
+            wide = term if wide is None else wide + term
+        arrive = wide[0:days, 0:reaches]
+        for k in range(1, groups):
+            arrive = arrive + wide[k * days : (k + 1) * days, k * reaches : (k + 1) * reaches]
         out_ref[...] = out_ref[...] + arrive
 
     inflow = out_ref[...]
@@ -176,56 +181,40 @@
     gain = coef_ref[1:2, :]
     c2 = coef_ref[2:3, :]
     lagged = jnp.zeros_like(c0)
-    rows = []
+    day_rows = []
     for t in range(days):
         if t > 0:
             lagged = inflow[t - 1 : t, :] + c2 * lagged
-        rows.append(c0 * inflow[t : t + 1, :] + gain * lagged)
-    discharge = jnp.concatenate(rows, axis=0)
+        day_rows.append(c0 * inflow[t : t + 1, :] + gain * lagged)
+    discharge = jnp.concatenate(day_rows, axis=0)
     out_ref[...] = discharge
 
     @pl.when(o < n_order - 1)
     def _():
         packed_val = None
         for part in split2(discharge):
-            term = lax.dot_general(send_ref[...], part, (((1,), (1,)), ((), ())),
+            for k in range(groups):
+                spread[k * days : (k + 1) * days, k * reaches : (k + 1) * reaches] = part
+            term = lax.dot_general(send_ref[...], spread[...], (((1,), (1,)), ((), ())),
                                    preferred_element_type=jnp.float32)
             packed_val = term if packed_val is None else packed_val + term
         packed[...] = packed_val
 
         def start(j, carry):
-            pltpu.make_async_remote_copy(
-                src_ref=packed.at[pl.ds(j * cap, cap)],
-                dst_ref=recv.at[pl.ds(b * cap, cap)],
-                send_sem=send_sem.at[j],
-                recv_sem=recv_sem.at[b],
-                device_id=(o + 1, j),
-                device_id_type=MESH,
-            ).start()
+            data_copy(j, b, o + 1).start()
             return carry
         lax.fori_loop(0, n_basin, start, 0)
 
         def finish(j, carry):
-            pltpu.make_async_remote_copy(
-                src_ref=packed.at[pl.ds(j * cap, cap)],
-                dst_ref=recv.at[pl.ds(b * cap, cap)],
-                send_sem=send_sem.at[j],
-                recv_sem=recv_sem.at[b],
-                device_id=(o + 1, j),
-                device_id_type=MESH,
-            ).wait_send()
+            data_copy(j, b, o + 1).wait_send()
+            target_copy(j, b, o + 1).wait_send()
             return carry
         lax.fori_loop(0, n_basin, finish, 0)
-
-        def finish_targets(j, carry):
-            target_copy(j, b).wait_send()
-            return carry
-        lax.fori_loop(0, n_basin, finish_targets, 0)
 
 
 def route_chain(runoff, coef, send_t, tgt, n_order, n_basin, cap):
     days, reaches = runoff.shape
-    slots = n_basin * cap
+    groups = cap // 8
     vmem = pl.BlockSpec(memory_space=pltpu.VMEM)
     return pl.pallas_call(
         functools.partial(chain_kernel, n_order, n_basin, cap),
@@ -233,10 +222,11 @@
         in_specs=[vmem] * 4,
         out_specs=vmem,
         scratch_shapes=[
-            pltpu.VMEM((slots, days), jnp.float32),
-            pltpu.VMEM((slots, days), jnp.float32),
-            pltpu.VMEM((slots, reaches), jnp.bfloat16),
-            pltpu.VMEM((slots, 1), jnp.int32),
+            pltpu.VMEM((n_basin * 8, groups * days), jnp.float32),
+            pltpu.VMEM((n_basin * 8, groups * days), jnp.float32),
+            pltpu.VMEM((n_basin * 8, groups * reaches), jnp.bfloat16),
+            pltpu.VMEM((n_basin * 8, groups), jnp.int32),
+            pltpu.VMEM((groups * days, groups * reaches), jnp.bfloat16),
             pltpu.SemaphoreType.DMA((n_basin,)),
             pltpu.SemaphoreType.DMA((n_basin,)),
             pltpu.SemaphoreType.DMA((n_basin,)),
@@ -265,10 +255,14 @@
     send_int = (
         flat_slot[:, None] == jnp.arange(slots, dtype=jnp.int32)[None, :]
     ).astype(jnp.int32)
-    sent_targets = (jnp.dot(drain_reach[:, 0] + 1, send_int) - 1).reshape(slots, 1)
+    groups_k = capacity // 8
+    sent_targets = (jnp.dot(drain_reach[:, 0] + 1, send_int) - 1).reshape(basins, groups_k, 8)
+    sent_targets = sent_targets.transpose(0, 2, 1).reshape(basins * 8, groups_k)
     send_t = (
         jnp.arange(slots, dtype=jnp.int32)[:, None] == flat_slot[None, :]
     ).astype(jnp.bfloat16)
+    send_t = send_t.reshape(basins, groups_k, 8, reach_count).transpose(0, 2, 1, 3)
+    send_t = send_t.reshape(basins * 8, groups_k * reach_count)
 
     denominator = travel_time * (1.0 - weight_x) + 0.5
     coeff_first = (0.5 - travel_time * weight_x) / denominator

time: 135 us -> 99.2 us (0.73); the launches traced: 132 us -> 98.8 us
  Pallas kernels: 117 us -> 85.5 us
    pallas_call x1, Pallas kernels: 98.5 us -> 66.8 us  [route_chain(): pl.pallas_call(functools.partial(chain_kernel, n_order, n_basin, cap), ou...]
    unnamed x9 -> x17, local copies, waits for them, and re-layouts: 3.72 us -> 3.75 us
where the time goes in v4:
time: 99.2 us; the launch traced here: 98.8 us
  Pallas kernels  85.5 us (86%)
  local copies, waits for them, and re-layouts  6.95 us (7%)
  other arithmetic  5.31 us (5%)
    pallas_call x1, Pallas kernels, route_chain(): pl.pallas_call(functools.partial(chain_kernel, n_order, n_basin, cap), ou...  66.8 us
    pallas_call x1, Pallas kernels, lstm_runoff(): pl.pallas_call(functools.partial(lstm_kernel, block), out_shape=jax.Shape...  18.7 us
    unnamed x17, local copies, waits for them, and re-layouts  3.75 us

profile of v4, /device:TPU:25, one launch (start us, length us, event | category | flops | bytes accessed | tf_op | source)
XLA Modules:
  0.0 98.8 jit_solution(18140856429901155362)
XLA Ops:
  0.0 0.7 add_divide_fusion
  0.7 0.1 scatter.11
  0.8 0.1 scatter.14.coef_ref
  0.9 0.7 fusion.4
  1.5 1.2 %reduce-window.6 = s32[32,4,128]{2,0,1:T(8,128)S(1)} reduce-window(s32[32,4,128]{2,0,1:T(8,128)S(1)} %fusion.4, s32[]{:T(128)} %constant.101.clone.1), window={size=1x1x128 pad=0_0x0_0x127_0}, to_apply=%region_0.0 | reduce-window | flops 2080768 | bytes 131076 | tf_op jit(solution)/shard_map/reduce-window
  2.7 0.2 slice_reduce_fusion
  3.0 0.8 fusion.3
  3.8 0.7 broadcast_add_fusion.1
  4.5 0.2 eq.78
  4.7 0.0 copy-start.1
  4.7 0.0 copy-start.5
  4.7 0.0 copy-start.3
  4.7 0.0 copy-start.4
  4.7 1.2 %compare_convert_fusion.send_ref = bf16[256,2048]{1,0:T(8,128)(2,1)} fusion(s32[256,2048]{1,0:T(8,128)S(1)} %bitcast.35, s32[2048]{0:T(1024)S(1)} %bitcast.39), kind=kLoop, calls=%fused_computation.1 | loop fusion | flops 1048576 | bytes 3153920 | tf_op jit(solution)/shard_map/convert_element_type | solution.py:263
  6.0 1.0 fusion
  7.0 0.1 reshape.148
  7.1 0.9 copy.16
  8.0 0.9 copy.13.bias_ref
  8.9 0.8 copy.12.w_in_ref
  9.6 0.7 copy.14.w_ro_ref
  10.4 18.7 %shard_map.91 = f32[32,1,512]{2,1,0:T(1,128)} custom-call(bf16[32,16,512]{2,1,0:T(8,128)(2,1)} %forc_ref.1, bf16[512,16]{1,0:T(8,128)(2,1)} %copy.12.w_in_ref, bf16[512,128]{1,0:T(8,128)(2,1)} %w_rec_ref.1, f32[512,1]{1,0:T(8,128)} %copy.13.bias_ref, f32[128,1]{1,0:T(8,128)} %copy.14.w_ro_ref), custom_call_target="tpu_custom_call" | custom-call | tf_op jit(solution)/shard_map/pallas_call | solution.py:71
  29.1 1.5 %copy.22 = f32[32,1,512]{2,0,1:T(8,128)} copy(f32[32,1,512]{2,1,0:T(1,128)} %shard_map.91) | data formatting | bytes 131072
  30.5 66.8 %shard_map.92 = f32[32,512]{1,0:T(8,128)} custom-call(f32[32,512]{1,0:T(8,128)} %bitcast.38, f32[8,512]{1,0:T(8,128)} %copy-done, bf16[256,2048]{1,0:T(8,128)(2,1)} %compare_convert_fusion.send_ref, s32[256,4]{1,0:T(8,128)} %bitcast.36), custom_call_target="tpu_custom_call" | custom-call | tf_op jit(solution)/shard_map/pallas_call | solution.py:219
  97.4 1.5 %copy.26 = f32[32,512]{1,0:T(8,128)} copy(f32[32,512]{1,0:T(8,128)} %shard_map.92) | data formatting | bytes 131072
  (16 shorter events, 0.1 us)
Async XLA Ops:
  0.8 5.1 %copy-start = (f32[8,512]{1,0:T(8,128)}, f32[8,512]{1,0:T(8,128)S(1)}, u32[]{:S(2)}) copy-start(f32[8,512]{1,0:T(8,128)S(1)} %scatter.14.coef_ref) | copy-start | bytes 49156
  4.7 1.3 %copy-start.1 = (s32[512,1]{0,1:T(1,128)S(1)}, s32[512,1]{0,1:T(1,128)}, u32[]{:S(2)}) copy-start(s32[512,1]{0,1:T(1,128)} %param.22) | copy-start | bytes 6148
  4.7 1.3 %copy-start.5 = (s32[512,1]{0,1:T(1,128)S(1)}, s32[512,1]{0,1:T(1,128)}, u32[]{:S(2)}) copy-start(s32[512,1]{0,1:T(1,128)} %param.23) | copy-start | bytes 6148
  4.7 3.3 %copy-start.3 = (f32[512]{0:T(512)S(1)}, f32[512]{0:T(512)}, u32[]{:S(2)}) copy-start(f32[512]{0:T(512)} %param.18) | copy-start | bytes 6148
  4.7 4.2 %copy-start.2 = (bf16[512,16]{0,1:T(8,128)(2,1)S(1)}, bf16[512,16]{0,1:T(8,128)(2,1)}, u32[]{:S(2)}) copy-start(bf16[512,16]{0,1:T(8,128)(2,1)} %param.16) | copy-start | bytes 49156
  4.7 4.9 %copy-start.4 = (f32[128]{0:T(128)S(1)}, f32[128]{0:T(128)}, u32[]{:S(2)}) copy-start(f32[128]{0:T(128)} %param.19) | copy-start | bytes 1540

commit v5 on v4

--- a/solution.py
+++ b/solution.py
@@ -166,11 +166,11 @@
             data_copy(j, j, o - 1).wait_recv()
             return carry
         lax.fori_loop(0, n_basin, arrived, 0)
-        wide = None
-        for part in split2(recv[...]):
-            term = lax.dot_general(part, table_ref[...], (((0,), (0,)), ((), ())),
-                                   preferred_element_type=jnp.float32)
-            wide = term if wide is None else wide + term
+        both = jnp.concatenate(split2(recv[...]), axis=1)
+        stacked = lax.dot_general(both, table_ref[...], (((0,), (0,)), ((), ())),
+                                  preferred_element_type=jnp.float32)
+        half = stacked.shape[0] // 2
+        wide = stacked[:half] + stacked[half:]
         arrive = wide[0:days, 0:reaches]
         for k in range(1, groups):
             arrive = arrive + wide[k * days : (k + 1) * days, k * reaches : (k + 1) * reaches]
@@ -191,14 +191,14 @@
 
     @pl.when(o < n_order - 1)
     def _():
-        packed_val = None
-        for part in split2(discharge):
+        for p, part in enumerate(split2(discharge)):
             for k in range(groups):
-                spread[k * days : (k + 1) * days, k * reaches : (k + 1) * reaches] = part
-            term = lax.dot_general(send_ref[...], spread[...], (((1,), (1,)), ((), ())),
-                                   preferred_element_type=jnp.float32)
-            packed_val = term if packed_val is None else packed_val + term
-        packed[...] = packed_val
+                top = (p * groups + k) * days
+                spread[top : top + days, k * reaches : (k + 1) * reaches] = part
+        stacked = lax.dot_general(send_ref[...], spread[...], (((1,), (1,)), ((), ())),
+                                  preferred_element_type=jnp.float32)
+        half = stacked.shape[1] // 2
+        packed[...] = stacked[:, :half] + stacked[:, half:]
 
         def start(j, carry):
             data_copy(j, b, o + 1).start()
@@ -226,7 +226,7 @@
             pltpu.VMEM((n_basin * 8, groups * days), jnp.float32),
             pltpu.VMEM((n_basin * 8, groups * reaches), jnp.bfloat16),
             pltpu.VMEM((n_basin * 8, groups), jnp.int32),
-            pltpu.VMEM((groups * days, groups * reaches), jnp.bfloat16),
+            pltpu.VMEM((2 * groups * days, groups * reaches), jnp.bfloat16),
             pltpu.SemaphoreType.DMA((n_basin,)),
             pltpu.SemaphoreType.DMA((n_basin,)),
             pltpu.SemaphoreType.DMA((n_basin,)),

time: 99.2 us -> 97.5 us (0.983)
  Pallas kernels: 85.5 us -> 83.9 us
    pallas_call x1, Pallas kernels: 66.8 us -> 65.2 us  [route_chain(): pl.pallas_call(functools.partial(chain_kernel, n_order, n_basin, cap), ou...]
where the time goes in v5:
time: 97.5 us; the launch traced here: 97.2 us
  Pallas kernels  83.9 us (86%)
  local copies, waits for them, and re-layouts  6.95 us (7%)
  other arithmetic  5.31 us (5%)
    pallas_call x1, Pallas kernels, route_chain(): pl.pallas_call(functools.partial(chain_kernel, n_order, n_basin, cap), ou...  65.2 us
    pallas_call x1, Pallas kernels, lstm_runoff(): pl.pallas_call(functools.partial(lstm_kernel, block), out_shape=jax.Shape...  18.7 us
    unnamed x17, local copies, waits for them, and re-layouts  3.75 us

profile of v5, /device:TPU:25, one launch (start us, length us, event | category | flops | bytes accessed | tf_op | source)
XLA Modules:
  0.0 97.2 jit_solution(4039711083201823572)
XLA Ops:
  0.0 0.7 add_divide_fusion
  0.7 0.1 scatter.11
  0.8 0.1 scatter.14.coef_ref
  0.9 0.7 fusion.4
  1.5 1.2 %reduce-window.6 = s32[32,4,128]{2,0,1:T(8,128)S(1)} reduce-window(s32[32,4,128]{2,0,1:T(8,128)S(1)} %fusion.4, s32[]{:T(128)} %constant.101.clone.1), window={size=1x1x128 pad=0_0x0_0x127_0}, to_apply=%region_0.0 | reduce-window | flops 2080768 | bytes 131076 | tf_op jit(solution)/shard_map/reduce-window
  2.7 0.2 slice_reduce_fusion
  3.0 0.8 fusion.3
  3.8 0.7 broadcast_add_fusion.1
  4.5 0.2 eq.78
  4.7 0.0 copy-start.1
  4.7 0.0 copy-start.5
  4.7 0.0 copy-start.3
  4.7 0.0 copy-start.4
  4.7 1.2 %compare_convert_fusion.send_ref = bf16[256,2048]{1,0:T(8,128)(2,1)} fusion(s32[256,2048]{1,0:T(8,128)S(1)} %bitcast.35, s32[2048]{0:T(1024)S(1)} %bitcast.39), kind=kLoop, calls=%fused_computation.1 | loop fusion | flops 1048576 | bytes 3153920 | tf_op jit(solution)/shard_map/convert_element_type | solution.py:263
  6.0 1.0 fusion
  7.0 0.1 reshape.148
  7.1 0.9 copy.16
  8.0 0.9 copy.13.bias_ref
  8.9 0.8 copy.12.w_in_ref
  9.6 0.7 copy.14.w_ro_ref
  10.4 18.7 %shard_map.91 = f32[32,1,512]{2,1,0:T(1,128)} custom-call(bf16[32,16,512]{2,1,0:T(8,128)(2,1)} %forc_ref.1, bf16[512,16]{1,0:T(8,128)(2,1)} %copy.12.w_in_ref, bf16[512,128]{1,0:T(8,128)(2,1)} %w_rec_ref.1, f32[512,1]{1,0:T(8,128)} %copy.13.bias_ref, f32[128,1]{1,0:T(8,128)} %copy.14.w_ro_ref), custom_call_target="tpu_custom_call" | custom-call | tf_op jit(solution)/shard_map/pallas_call | solution.py:71
  29.1 1.5 %copy.22 = f32[32,1,512]{2,0,1:T(8,128)} copy(f32[32,1,512]{2,1,0:T(1,128)} %shard_map.91) | data formatting | bytes 131072
  30.5 65.2 %shard_map.92 = f32[32,512]{1,0:T(8,128)} custom-call(f32[32,512]{1,0:T(8,128)} %bitcast.38, f32[8,512]{1,0:T(8,128)} %copy-done, bf16[256,2048]{1,0:T(8,128)(2,1)} %compare_convert_fusion.send_ref, s32[256,4]{1,0:T(8,128)} %bitcast.36), custom_call_target="tpu_custom_call" | custom-call | tf_op jit(solution)/shard_map/pallas_call | solution.py:219
  95.8 1.5 %copy.26 = f32[32,512]{1,0:T(8,128)} copy(f32[32,512]{1,0:T(8,128)} %shard_map.92) | data formatting | bytes 131072
  (16 shorter events, 0.1 us)
Async XLA Ops:
  0.8 5.1 %copy-start = (f32[8,512]{1,0:T(8,128)}, f32[8,512]{1,0:T(8,128)S(1)}, u32[]{:S(2)}) copy-start(f32[8,512]{1,0:T(8,128)S(1)} %scatter.14.coef_ref) | copy-start | bytes 49156
  4.7 1.3 %copy-start.1 = (s32[512,1]{0,1:T(1,128)S(1)}, s32[512,1]{0,1:T(1,128)}, u32[]{:S(2)}) copy-start(s32[512,1]{0,1:T(1,128)} %param.22) | copy-start | bytes 6148
  4.7 1.3 %copy-start.5 = (s32[512,1]{0,1:T(1,128)S(1)}, s32[512,1]{0,1:T(1,128)}, u32[]{:S(2)}) copy-start(s32[512,1]{0,1:T(1,128)} %param.23) | copy-start | bytes 6148
  4.7 3.3 %copy-start.3 = (f32[512]{0:T(512)S(1)}, f32[512]{0:T(512)}, u32[]{:S(2)}) copy-start(f32[512]{0:T(512)} %param.18) | copy-start | bytes 6148
  4.7 4.2 %copy-start.2 = (bf16[512,16]{0,1:T(8,128)(2,1)S(1)}, bf16[512,16]{0,1:T(8,128)(2,1)}, u32[]{:S(2)}) copy-start(bf16[512,16]{0,1:T(8,128)(2,1)} %param.16) | copy-start | bytes 49156
  4.7 4.9 %copy-start.4 = (f32[128]{0:T(128)S(1)}, f32[128]{0:T(128)}, u32[]{:S(2)}) copy-start(f32[128]{0:T(128)} %param.19) | copy-start | bytes 1540

commit v6 on v5

--- a/solution.py
+++ b/solution.py
@@ -86,7 +86,19 @@
     return hi, lo
 
 
-def chain_kernel(n_order, n_basin, cap, runoff_ref, coef_ref, send_ref, tgt_ref, out_ref,
+def route_days(inflow, coef):
+    days = inflow.shape[0]
+    c0, gain, c2 = coef
+    lagged = jnp.zeros_like(c0)
+    day_rows = []
+    for t in range(days):
+        if t > 0:
+            lagged = inflow[t - 1 : t, :] + c2 * lagged
+        day_rows.append(c0 * inflow[t : t + 1, :] + gain * lagged)
+    return jnp.concatenate(day_rows, axis=0)
+
+
+def chain_kernel(n_order, n_basin, cap, runoff_ref, tt_ref, wx_ref, send_ref, tgt_ref, out_ref,
                  packed, recv, table_ref, tgt_recv, spread, send_sem, recv_sem, tsend_sem, trecv_sem):
     o = lax.axis_index("order")
     b = lax.axis_index("basin")
@@ -109,6 +121,32 @@
     @pl.when(o < n_order - 1)
     def _():
         greet(o + 1)
+
+    travel = tt_ref[...]
+    weight = wx_ref[...]
+    denominator = travel * (1.0 - weight) + 0.5
+    coeff_first = (0.5 - travel * weight) / denominator
+    coeff_second = (0.5 + travel * weight) / denominator
+    recession = (travel * (1.0 - weight) - 0.5) / denominator
+    coef = (coeff_first, coeff_first * recession + coeff_second, recession)
+
+    def pack(discharge):
+        for p, part in enumerate(split2(discharge)):
+            for k in range(groups):
+                top = (p * groups + k) * days
+                spread[top : top + days, k * reaches : (k + 1) * reaches] = part
+        stacked = lax.dot_general(send_ref[...], spread[...], (((1,), (1,)), ((), ())),
+                                  preferred_element_type=jnp.float32)
+        half = stacked.shape[1] // 2
+        packed[...] = stacked[:, :half] + stacked[:, half:]
+
+    spread[...] = jnp.zeros_like(spread)
+
+    @pl.when(o == 0)
+    def _():
+        discharge = route_days(runoff_ref[...], coef)
+        out_ref[...] = discharge
+        pack(discharge)
 
     at_end = jnp.logical_or(o == 0, o == n_order - 1)
 
@@ -147,9 +185,6 @@
             return carry
         lax.fori_loop(0, n_basin, start, 0)
 
-    spread[...] = jnp.zeros_like(spread)
-    out_ref[...] = runoff_ref[...]
-
     @pl.when(o > 0)
     def _():
         def got(j, carry):
@@ -174,32 +209,15 @@
         arrive = wide[0:days, 0:reaches]
         for k in range(1, groups):
             arrive = arrive + wide[k * days : (k + 1) * days, k * reaches : (k + 1) * reaches]
-        out_ref[...] = out_ref[...] + arrive
-
-    inflow = out_ref[...]
-    c0 = coef_ref[0:1, :]
-    gain = coef_ref[1:2, :]
-    c2 = coef_ref[2:3, :]
-    lagged = jnp.zeros_like(c0)
-    day_rows = []
-    for t in range(days):
-        if t > 0:
-            lagged = inflow[t - 1 : t, :] + c2 * lagged
-        day_rows.append(c0 * inflow[t : t + 1, :] + gain * lagged)
-    discharge = jnp.concatenate(day_rows, axis=0)
-    out_ref[...] = discharge
+        discharge = route_days(runoff_ref[...] + arrive, coef)
+        out_ref[...] = discharge
+
+        @pl.when(o < n_order - 1)
+        def _():
+            pack(discharge)
 
     @pl.when(o < n_order - 1)
     def _():
-        for p, part in enumerate(split2(discharge)):
-            for k in range(groups):
-                top = (p * groups + k) * days
-                spread[top : top + days, k * reaches : (k + 1) * reaches] = part
-        stacked = lax.dot_general(send_ref[...], spread[...], (((1,), (1,)), ((), ())),
-                                  preferred_element_type=jnp.float32)
-        half = stacked.shape[1] // 2
-        packed[...] = stacked[:, :half] + stacked[:, half:]
-
         def start(j, carry):
             data_copy(j, b, o + 1).start()
             return carry
@@ -212,14 +230,14 @@
         lax.fori_loop(0, n_basin, finish, 0)
 
 
-def route_chain(runoff, coef, send_t, tgt, n_order, n_basin, cap):
+def route_chain(runoff, travel_time, weight_x, send_t, tgt, n_order, n_basin, cap):
     days, reaches = runoff.shape
     groups = cap // 8
     vmem = pl.BlockSpec(memory_space=pltpu.VMEM)
     return pl.pallas_call(
         functools.partial(chain_kernel, n_order, n_basin, cap),
         out_shape=jax.ShapeDtypeStruct((days, reaches), jnp.float32),
-        in_specs=[vmem] * 4,
+        in_specs=[vmem] * 5,
         out_specs=vmem,
         scratch_shapes=[
             pltpu.VMEM((n_basin * 8, groups * days), jnp.float32),
@@ -233,7 +251,7 @@
             pltpu.SemaphoreType.DMA((n_basin,)),
         ],
         compiler_params=pltpu.CompilerParams(collective_id=0, has_side_effects=True),
-    )(runoff, coef, send_t, tgt)
+    )(runoff, travel_time.reshape(1, reaches), weight_x.reshape(1, reaches), send_t, tgt)
 
 
 def per_device(
@@ -264,16 +282,8 @@
     send_t = send_t.reshape(basins, groups_k, 8, reach_count).transpose(0, 2, 1, 3)
     send_t = send_t.reshape(basins * 8, groups_k * reach_count)
 
-    denominator = travel_time * (1.0 - weight_x) + 0.5
-    coeff_first = (0.5 - travel_time * weight_x) / denominator
-    coeff_second = (0.5 + travel_time * weight_x) / denominator
-    recession = (travel_time * (1.0 - weight_x) - 0.5) / denominator
-    gain = coeff_first * recession + coeff_second
-    coef = jnp.zeros((8, reach_count), jnp.float32)
-    coef = coef.at[0].set(coeff_first).at[1].set(gain).at[2].set(recession)
-
     runoff = lstm_runoff(forcings, w_input, w_recur, gate_bias, w_runoff)
-    return route_chain(runoff, coef, send_t, sent_targets, groups, basins, capacity)
+    return route_chain(runoff, travel_time, weight_x, send_t, sent_targets, groups, basins, capacity)
 
 
 def solution(mesh):

time: 97.5 us -> 96.7 us (level)
    unnamed x17 -> x15, local copies, waits for them, and re-layouts: 3.75 us -> 3.75 us
where the time goes in v6:
time: 96.7 us; the launch traced here: 96.5 us
  Pallas kernels  84 us (87%)
  local copies, waits for them, and re-layouts  6.82 us (7%)
  other arithmetic  4.6 us (5%)
    pallas_call x1, Pallas kernels, route_chain(): pl.pallas_call(functools.partial(chain_kernel, n_order, n_basin, cap), ou...  65.4 us
    pallas_call x1, Pallas kernels, lstm_runoff(): pl.pallas_call(functools.partial(lstm_kernel, block), out_shape=jax.Shape...  18.6 us
    unnamed x15, local copies, waits for them, and re-layouts  3.75 us

profile of v6, /device:TPU:25, one launch (start us, length us, event | category | flops | bytes accessed | tf_op | source)
XLA Modules:
  0.0 96.5 jit_solution(8389896812520682273)
XLA Ops:
  0.0 0.7 fusion.4
  0.7 1.2 %reduce-window.6 = s32[32,4,128]{2,0,1:T(8,128)S(1)} reduce-window(s32[32,4,128]{2,0,1:T(8,128)S(1)} %fusion.4, s32[]{:T(128)} %constant.14.clone.1), window={size=1x1x128 pad=0_0x0_0x127_0}, to_apply=%region_0.0 | reduce-window | flops 2080768 | bytes 131076 | tf_op jit(solution)/shard_map/reduce-window
  1.8 0.2 slice_reduce_fusion
  2.1 0.8 fusion.3
  2.9 0.7 broadcast_add_fusion.1
  3.6 0.2 eq.78
  3.8 0.0 copy-start
  3.8 0.0 copy-start.4
  3.8 0.0 copy-start.2
  3.9 0.0 copy-start.1
  3.9 0.0 copy-start.3
  3.9 1.2 %compare_convert_fusion.send_ref = bf16[256,2048]{1,0:T(8,128)(2,1)} fusion(s32[256,2048]{1,0:T(8,128)S(1)} %bitcast.34, s32[2048]{0:T(1024)S(1)} %bitcast.38), kind=kLoop, calls=%fused_computation.1 | loop fusion | flops 1048576 | bytes 3153920 | tf_op jit(solution)/shard_map/convert_element_type | solution.py:281
  5.1 0.0 copy-done
  5.1 0.0 copy-done.4
  5.1 1.0 fusion
  6.1 0.1 reshape.77
  6.2 0.9 copy.16
  7.1 0.9 copy.13.bias_ref
  8.0 0.8 copy.12.w_in_ref
  8.8 0.7 copy.14.w_ro_ref
  9.5 18.6 %shard_map.91 = f32[32,1,512]{2,1,0:T(1,128)} custom-call(bf16[32,16,512]{2,1,0:T(8,128)(2,1)} %forc_ref.1, bf16[512,16]{1,0:T(8,128)(2,1)} %copy.12.w_in_ref, bf16[512,128]{1,0:T(8,128)(2,1)} %w_rec_ref.1, f32[512,1]{1,0:T(8,128)} %copy.13.bias_ref, f32[128,1]{1,0:T(8,128)} %copy.14.w_ro_ref), custom_call_target="tpu_custom_call" | custom-call | tf_op jit(solution)/shard_map/pallas_call | solution.py:71
  28.1 1.5 %copy.22 = f32[32,1,512]{2,0,1:T(8,128)} copy(f32[32,1,512]{2,1,0:T(1,128)} %shard_map.91) | data formatting | bytes 131072
  29.5 65.4 %shard_map.92 = f32[32,512]{1,0:T(8,128)} custom-call(f32[32,512]{1,0:T(8,128)} %bitcast.36, f32[1,512]{1,0:T(1,128)} %bitcast.45, f32[1,512]{1,0:T(1,128)} %bitcast.46, bf16[256,2048]{1,0:T(8,128)(2,1)} %compare_convert_fusion.send_ref, s32[256,4]{1,0:T(8,128)} %bitcast.35), custom_call_target="tpu_custom_call" | custom-call | tf_op jit(solution)/shard_map/pallas_call | solution.py:237
  95.0 1.5 %copy.24 = f32[32,512]{1,0:T(8,128)} copy(f32[32,512]{1,0:T(8,128)} %shard_map.92) | data formatting | bytes 131072
  (10 shorter events, 0.1 us)
Async XLA Ops:
  3.8 1.3 %copy-start = (s32[512,1]{0,1:T(1,128)S(1)}, s32[512,1]{0,1:T(1,128)}, u32[]{:S(2)}) copy-start(s32[512,1]{0,1:T(1,128)} %param.16) | copy-start | bytes 6148
  3.8 1.3 %copy-start.4 = (s32[512,1]{0,1:T(1,128)S(1)}, s32[512,1]{0,1:T(1,128)}, u32[]{:S(2)}) copy-start(s32[512,1]{0,1:T(1,128)} %param.17) | copy-start | bytes 6148
  3.8 3.3 %copy-start.2 = (f32[512]{0:T(512)S(1)}, f32[512]{0:T(512)}, u32[]{:S(2)}) copy-start(f32[512]{0:T(512)} %param.12) | copy-start | bytes 6148
  3.9 4.1 %copy-start.1 = (bf16[512,16]{0,1:T(8,128)(2,1)S(1)}, bf16[512,16]{0,1:T(8,128)(2,1)}, u32[]{:S(2)}) copy-start(bf16[512,16]{0,1:T(8,128)(2,1)} %param.10) | copy-start | bytes 49156
  3.9 4.9 %copy-start.3 = (f32[128]{0:T(128)S(1)}, f32[128]{0:T(128)}, u32[]{:S(2)}) copy-start(f32[128]{0:T(128)} %param.13) | copy-start | bytes 1540

commit v7 on v6

--- a/solution.py
+++ b/solution.py
@@ -34,34 +34,44 @@
     return lax.scan(one_day, lstm_state, day_block)
 
 
+def half_tanh_sigmoid(x):
+    return 0.5 + 0.5 * jnp.tanh(0.5 * x)
+
+
 def lstm_kernel(block, forc_ref, w_in_ref, w_rec_ref, bias_ref, w_ro_ref, out_ref, h_scr, c_scr):
     days = forc_ref.shape[0]
     units = w_rec_ref.shape[1]
-    reaches = out_ref.shape[2]
+    reaches = out_ref.shape[1]
+    rows = 8
     h_scr[...] = jnp.zeros_like(h_scr)
     c_scr[...] = jnp.zeros_like(c_scr)
 
-    def day(t, carry):
+    def step(t, cols):
+        gates = (
+            jnp.dot(w_in_ref[...], forc_ref[t, :, cols], preferred_element_type=jnp.float32)
+            + jnp.dot(w_rec_ref[...], h_scr[:, cols], preferred_element_type=jnp.float32)
+            + bias_ref[...]
+        )
+        ingate = half_tanh_sigmoid(gates[:units])
+        forget = half_tanh_sigmoid(gates[units : 2 * units])
+        candidate = jnp.tanh(gates[2 * units : 3 * units])
+        outgate = half_tanh_sigmoid(gates[3 * units :])
+        memory = forget * c_scr[:, cols] + ingate * candidate
+        hidden = (outgate * jnp.tanh(memory)).astype(jnp.bfloat16)
+        c_scr[:, cols] = memory
+        h_scr[:, cols] = hidden
+        z = jnp.sum(w_ro_ref[...] * hidden.astype(jnp.float32), axis=0, keepdims=True)
+        return jnp.maximum(z, 0.0) + jnp.log1p(jnp.exp(-jnp.abs(z)))
+
+    def week(w, carry):
+        first = pl.multiple_of(w * rows, rows)
         for j in range(reaches // block):
             cols = pl.ds(j * block, block)
-            gates = (
-                jnp.dot(w_in_ref[...], forc_ref[t, :, cols], preferred_element_type=jnp.float32)
-                + jnp.dot(w_rec_ref[...], h_scr[:, cols], preferred_element_type=jnp.float32)
-                + bias_ref[...]
-            )
-            ingate = jax.nn.sigmoid(gates[:units])
-            forget = jax.nn.sigmoid(gates[units : 2 * units])
-            candidate = jnp.tanh(gates[2 * units : 3 * units])
-            outgate = jax.nn.sigmoid(gates[3 * units :])
-            memory = forget * c_scr[:, cols] + ingate * candidate
-            hidden = (outgate * jnp.tanh(memory)).astype(jnp.bfloat16)
-            c_scr[:, cols] = memory
-            h_scr[:, cols] = hidden
-            z = jnp.sum(w_ro_ref[...] * hidden.astype(jnp.float32), axis=0, keepdims=True)
-            out_ref[t, :, cols] = jnp.maximum(z, 0.0) + jnp.log1p(jnp.exp(-jnp.abs(z)))
+            runoff = [step(first + k, cols) for k in range(rows)]
+            out_ref[pl.ds(first, rows), cols] = jnp.concatenate(runoff, axis=0)
         return carry
 
-    lax.fori_loop(0, days, day, 0)
+    lax.fori_loop(0, days // rows, week, 0)
 
 
 def lstm_runoff(forcings, w_input, w_recur, gate_bias, w_runoff, block=128):
@@ -70,14 +80,14 @@
     vmem = pl.BlockSpec(memory_space=pltpu.VMEM)
     return pl.pallas_call(
         functools.partial(lstm_kernel, block),
-        out_shape=jax.ShapeDtypeStruct((days, 1, reaches), jnp.float32),
+        out_shape=jax.ShapeDtypeStruct((days, reaches), jnp.float32),
         in_specs=[vmem] * 5,
         out_specs=vmem,
         scratch_shapes=[
             pltpu.VMEM((units, reaches), jnp.bfloat16),
             pltpu.VMEM((units, reaches), jnp.float32),
         ],
-    )(forcings, w_input, w_recur, gate_bias[:, None], w_runoff[:, None]).reshape(days, reaches)
+    )(forcings, w_input, w_recur, gate_bias[:, None], w_runoff[:, None])
 
 
 def split2(x):

time: 96.7 us -> 109 us (1.13)
  Pallas kernels: 84 us -> 98.2 us
  local copies, waits for them, and re-layouts: 6.82 us -> 5.35 us
    pallas_call x1, Pallas kernels: 18.6 us -> 33.1 us  [lstm_runoff(): pl.pallas_call(functools.partial(lstm_kernel, block), out_shape=jax.Shape...]
    unnamed x15 -> x14, local copies, waits for them, and re-layouts: 3.75 us -> 2.27 us
where the time goes in v7:
time: 109 us
  Pallas kernels  98.2 us (90%)
  local copies, waits for them, and re-layouts  5.35 us (5%)
  other arithmetic  4.6 us (4%)
    pallas_call x1, Pallas kernels, route_chain(): pl.pallas_call(functools.partial(chain_kernel, n_order, n_basin, cap), ou...  65.1 us
    pallas_call x1, Pallas kernels, lstm_runoff(): pl.pallas_call(functools.partial(lstm_kernel, block), out_shape=jax.Shape...  33.1 us
    unnamed x14, local copies, waits for them, and re-layouts  2.27 us

profile of v7, /device:TPU:25, one launch (start us, length us, event | category | flops | bytes accessed | tf_op | source)
XLA Modules:
  0.0 109.2 jit_solution(10466099538419232897)
XLA Ops:
  0.0 0.7 fusion.4
  0.7 1.2 %reduce-window.6 = s32[32,4,128]{2,0,1:T(8,128)S(1)} reduce-window(s32[32,4,128]{2,0,1:T(8,128)S(1)} %fusion.4, s32[]{:T(128)} %constant.14.clone.1), window={size=1x1x128 pad=0_0x0_0x127_0}, to_apply=%region_0.0 | reduce-window | flops 2080768 | bytes 131076 | tf_op jit(solution)/shard_map/reduce-window
  1.8 0.2 slice_reduce_fusion
  2.1 0.8 fusion.3
  2.9 0.7 broadcast_add_fusion.1
  3.6 0.2 eq.78
  3.8 0.0 copy-start
  3.8 0.0 copy-start.4
  3.8 0.0 copy-start.2
  3.9 0.0 copy-start.1
  3.9 0.0 copy-start.3
  3.9 1.2 %compare_convert_fusion.send_ref = bf16[256,2048]{1,0:T(8,128)(2,1)} fusion(s32[256,2048]{1,0:T(8,128)S(1)} %bitcast.31, s32[2048]{0:T(1024)S(1)} %bitcast.34), kind=kLoop, calls=%fused_computation.1 | loop fusion | flops 1048576 | bytes 3153920 | tf_op jit(solution)/shard_map/convert_element_type | solution.py:291
  5.1 0.0 copy-done
  5.1 0.0 copy-done.4
  5.1 1.0 fusion
  6.1 0.1 reshape.73
  6.2 0.9 copy.16
  7.1 0.0 copy-done.2
  7.1 0.9 copy.13.bias_ref
  8.0 0.8 copy.12.w_in_ref
  8.8 0.7 copy.14.w_ro_ref
  9.5 33.1 %shard_map.91.runoff_ref = f32[32,512]{1,0:T(8,128)} custom-call(bf16[32,16,512]{2,1,0:T(8,128)(2,1)} %forc_ref.1, bf16[512,16]{1,0:T(8,128)(2,1)} %copy.12.w_in_ref, bf16[512,128]{1,0:T(8,128)(2,1)} %w_rec_ref.1, f32[512,1]{1,0:T(8,128)} %copy.13.bias_ref, f32[128,1]{1,0:T(8,128)} %copy.14.w_ro_ref), custom_call_target="tpu_custom_call" | custom-call | tf_op jit(solution)/shard_map/pallas_call | solution.py:81
  42.6 65.1 %shard_map.92 = f32[32,512]{1,0:T(8,128)} custom-call(f32[32,512]{1,0:T(8,128)} %shard_map.91.runoff_ref, f32[1,512]{1,0:T(1,128)} %bitcast.41, f32[1,512]{1,0:T(1,128)} %bitcast.42, bf16[256,2048]{1,0:T(8,128)(2,1)} %compare_convert_fusion.send_ref, s32[256,4]{1,0:T(8,128)} %bitcast.32), custom_call_target="tpu_custom_call" | custom-call | tf_op jit(solution)/shard_map/pallas_call | solution.py:247
  107.7 1.5 %copy.21 = f32[32,512]{1,0:T(8,128)} copy(f32[32,512]{1,0:T(8,128)} %shard_map.92) | data formatting | bytes 131072
  (9 shorter events, 0.1 us)
Async XLA Ops:
  3.8 1.3 %copy-start = (s32[512,1]{0,1:T(1,128)S(1)}, s32[512,1]{0,1:T(1,128)}, u32[]{:S(2)}) copy-start(s32[512,1]{0,1:T(1,128)} %param.16) | copy-start | bytes 6148
  3.8 1.3 %copy-start.4 = (s32[512,1]{0,1:T(1,128)S(1)}, s32[512,1]{0,1:T(1,128)}, u32[]{:S(2)}) copy-start(s32[512,1]{0,1:T(1,128)} %param.17) | copy-start | bytes 6148
  3.8 3.3 %copy-start.2 = (f32[512]{0:T(512)S(1)}, f32[512]{0:T(512)}, u32[]{:S(2)}) copy-start(f32[512]{0:T(512)} %param.12) | copy-start | bytes 6148
  3.9 4.1 %copy-start.1 = (bf16[512,16]{0,1:T(8,128)(2,1)S(1)}, bf16[512,16]{0,1:T(8,128)(2,1)}, u32[]{:S(2)}) copy-start(bf16[512,16]{0,1:T(8,128)(2,1)} %param.10) | copy-start | bytes 49156
  3.9 4.9 %copy-start.3 = (f32[128]{0:T(128)S(1)}, f32[128]{0:T(128)}, u32[]{:S(2)}) copy-start(f32[128]{0:T(128)} %param.13) | copy-start | bytes 1540

commit v8 on v7

--- a/solution.py
+++ b/solution.py
@@ -38,11 +38,10 @@
     return 0.5 + 0.5 * jnp.tanh(0.5 * x)
 
 
-def lstm_kernel(block, forc_ref, w_in_ref, w_rec_ref, bias_ref, w_ro_ref, out_ref, h_scr, c_scr):
+def lstm_kernel(block, forc_ref, w_in_ref, w_rec_ref, bias_ref, w_ro_ref, out_ref, h_scr, c_scr, run_scr):
     days = forc_ref.shape[0]
     units = w_rec_ref.shape[1]
     reaches = out_ref.shape[1]
-    rows = 8
     h_scr[...] = jnp.zeros_like(h_scr)
     c_scr[...] = jnp.zeros_like(c_scr)
 
@@ -63,15 +62,15 @@
         z = jnp.sum(w_ro_ref[...] * hidden.astype(jnp.float32), axis=0, keepdims=True)
         return jnp.maximum(z, 0.0) + jnp.log1p(jnp.exp(-jnp.abs(z)))
 
-    def week(w, carry):
-        first = pl.multiple_of(w * rows, rows)
+    def day(t, carry):
         for j in range(reaches // block):
             cols = pl.ds(j * block, block)
-            runoff = [step(first + k, cols) for k in range(rows)]
-            out_ref[pl.ds(first, rows), cols] = jnp.concatenate(runoff, axis=0)
+            run_scr[t, :, cols] = step(t, cols)
         return carry
 
-    lax.fori_loop(0, days // rows, week, 0)
+    lax.fori_loop(0, days, day, 0)
+    for t in range(days):
+        out_ref[t : t + 1, :] = run_scr[t]
 
 
 def lstm_runoff(forcings, w_input, w_recur, gate_bias, w_runoff, block=128):
@@ -86,6 +85,7 @@
         scratch_shapes=[
             pltpu.VMEM((units, reaches), jnp.bfloat16),
             pltpu.VMEM((units, reaches), jnp.float32),
+            pltpu.VMEM((days, 1, reaches), jnp.float32),
         ],
     )(forcings, w_input, w_recur, gate_bias[:, None], w_runoff[:, None])
 

time: 109 us -> 95.1 us (0.87)
  Pallas kernels: 98.2 us -> 83.9 us
    pallas_call x1, Pallas kernels: 33.1 us -> 18.7 us  [lstm_runoff(): pl.pallas_call(functools.partial(lstm_kernel, block), out_shape=jax.Shape...]
where the time goes in v8:
time: 95.1 us; the launch traced here: 94.9 us
  Pallas kernels  83.9 us (88%)
  local copies, waits for them, and re-layouts  5.35 us (6%)
  other arithmetic  4.6 us (5%)
  matrix products  0.96 us (1%)
    pallas_call x1, Pallas kernels, route_chain(): pl.pallas_call(functools.partial(chain_kernel, n_order, n_basin, cap), ou...  65.2 us
    pallas_call x1, Pallas kernels, lstm_runoff(): pl.pallas_call(functools.partial(lstm_kernel, block), out_shape=jax.Shape...  18.7 us
    unnamed x14, local copies, waits for them, and re-layouts  2.27 us

profile of v8, /device:TPU:25, one launch (start us, length us, event | category | flops | bytes accessed | tf_op | source)
XLA Modules:
  0.0 94.9 jit_solution(3411463092969399823)
XLA Ops:
  0.0 0.7 fusion.4
  0.7 1.2 %reduce-window.6 = s32[32,4,128]{2,0,1:T(8,128)S(1)} reduce-window(s32[32,4,128]{2,0,1:T(8,128)S(1)} %fusion.4, s32[]{:T(128)} %constant.14.clone.1), window={size=1x1x128 pad=0_0x0_0x127_0}, to_apply=%region_0.0 | reduce-window | flops 2080768 | bytes 131076 | tf_op jit(solution)/shard_map/reduce-window
  1.8 0.2 slice_reduce_fusion
  2.1 0.8 fusion.3
  2.9 0.7 broadcast_add_fusion.1
  3.6 0.2 eq.78
  3.8 0.0 copy-start
  3.8 0.0 copy-start.4
  3.8 0.0 copy-start.2
  3.9 0.0 copy-start.1
  3.9 0.0 copy-start.3
  3.9 1.2 %compare_convert_fusion.send_ref = bf16[256,2048]{1,0:T(8,128)(2,1)} fusion(s32[256,2048]{1,0:T(8,128)S(1)} %bitcast.31, s32[2048]{0:T(1024)S(1)} %bitcast.34), kind=kLoop, calls=%fused_computation.1 | loop fusion | flops 1048576 | bytes 3153920 | tf_op jit(solution)/shard_map/convert_element_type | solution.py:291
  5.1 0.0 copy-done
  5.1 0.0 copy-done.4
  5.1 1.0 %fusion = s32[1,1024]{1,0:T(1,128)S(1)} fusion(s32[512]{0:T(512)S(1)} %bitcast.43, s32[512,1]{0,1:T(1,128)S(1)} %copy-done.4), kind=kOutput, calls=%fused_computation.2 | convolution fusion | flops 1573376 | bytes 8192 | tf_op jit(solution)/shard_map/dot_general | solution.py:287
  6.1 0.1 reshape.73
  6.2 0.9 copy.16
  7.1 0.0 copy-done.2
  7.1 0.9 copy.13.bias_ref
  8.0 0.8 copy.12.w_in_ref
  8.8 0.7 copy.14.w_ro_ref
  9.5 18.7 %shard_map.91.runoff_ref = f32[32,512]{1,0:T(8,128)} custom-call(bf16[32,16,512]{2,1,0:T(8,128)(2,1)} %forc_ref.1, bf16[512,16]{1,0:T(8,128)(2,1)} %copy.12.w_in_ref, bf16[512,128]{1,0:T(8,128)(2,1)} %w_rec_ref.1, f32[512,1]{1,0:T(8,128)} %copy.13.bias_ref, f32[128,1]{1,0:T(8,128)} %copy.14.w_ro_ref), custom_call_target="tpu_custom_call" | custom-call | tf_op jit(solution)/shard_map/pallas_call | solution.py:80
  28.2 65.2 %shard_map.92 = f32[32,512]{1,0:T(8,128)} custom-call(f32[32,512]{1,0:T(8,128)} %shard_map.91.runoff_ref, f32[1,512]{1,0:T(1,128)} %bitcast.41, f32[1,512]{1,0:T(1,128)} %bitcast.42, bf16[256,2048]{1,0:T(8,128)(2,1)} %compare_convert_fusion.send_ref, s32[256,4]{1,0:T(8,128)} %bitcast.32), custom_call_target="tpu_custom_call" | custom-call | tf_op jit(solution)/shard_map/pallas_call | solution.py:247
  93.4 1.5 %copy.21 = f32[32,512]{1,0:T(8,128)} copy(f32[32,512]{1,0:T(8,128)} %shard_map.92) | data formatting | bytes 131072
  (9 shorter events, 0.1 us)
Async XLA Ops:
  3.8 1.3 %copy-start = (s32[512,1]{0,1:T(1,128)S(1)}, s32[512,1]{0,1:T(1,128)}, u32[]{:S(2)}) copy-start(s32[512,1]{0,1:T(1,128)} %param.16) | copy-start | bytes 6148
  3.8 1.3 %copy-start.4 = (s32[512,1]{0,1:T(1,128)S(1)}, s32[512,1]{0,1:T(1,128)}, u32[]{:S(2)}) copy-start(s32[512,1]{0,1:T(1,128)} %param.17) | copy-start | bytes 6148
  3.8 3.3 %copy-start.2 = (f32[512]{0:T(512)S(1)}, f32[512]{0:T(512)}, u32[]{:S(2)}) copy-start(f32[512]{0:T(512)} %param.12) | copy-start | bytes 6148
  3.9 4.1 %copy-start.1 = (bf16[512,16]{0,1:T(8,128)(2,1)S(1)}, bf16[512,16]{0,1:T(8,128)(2,1)}, u32[]{:S(2)}) copy-start(bf16[512,16]{0,1:T(8,128)(2,1)} %param.10) | copy-start | bytes 49156
  3.9 4.9 %copy-start.3 = (f32[128]{0:T(128)S(1)}, f32[128]{0:T(128)}, u32[]{:S(2)}) copy-start(f32[128]{0:T(128)} %param.13) | copy-start | bytes 1540

commit v9 on v8

--- a/solution.py
+++ b/solution.py
@@ -73,7 +73,7 @@
         out_ref[t : t + 1, :] = run_scr[t]
 
 
-def lstm_runoff(forcings, w_input, w_recur, gate_bias, w_runoff, block=128):
+def lstm_runoff(forcings, w_input, w_recur, gate_bias, w_runoff, block=256):
     days, _, reaches = forcings.shape
     units = w_recur.shape[1]
     vmem = pl.BlockSpec(memory_space=pltpu.VMEM)

time: 95.1 us -> 96.4 us (1.014)
  Pallas kernels: 83.9 us -> 85.2 us
    pallas_call x1, Pallas kernels: 18.7 us -> 20.1 us  [lstm_runoff(): pl.pallas_call(functools.partial(lstm_kernel, block), out_shape=jax.Shape...]
where the time goes in v9:
time: 96.4 us; the launch traced here: 96.2 us
  Pallas kernels  85.2 us (88%)
  local copies, waits for them, and re-layouts  5.35 us (6%)
  other arithmetic  4.6 us (5%)
    pallas_call x1, Pallas kernels, route_chain(): pl.pallas_call(functools.partial(chain_kernel, n_order, n_basin, cap), ou...  65.1 us
    pallas_call x1, Pallas kernels, lstm_runoff(): pl.pallas_call(functools.partial(lstm_kernel, block), out_shape=jax.Shape...  20.1 us
    unnamed x14, local copies, waits for them, and re-layouts  2.27 us

profile of v9, /device:TPU:25, one launch (start us, length us, event | category | flops | bytes accessed | tf_op | source)
XLA Modules:
  0.0 96.2 jit_solution(8045269982616784694)
XLA Ops:
  0.0 0.7 fusion.4
  0.7 1.2 %reduce-window.6 = s32[32,4,128]{2,0,1:T(8,128)S(1)} reduce-window(s32[32,4,128]{2,0,1:T(8,128)S(1)} %fusion.4, s32[]{:T(128)} %constant.14.clone.1), window={size=1x1x128 pad=0_0x0_0x127_0}, to_apply=%region_0.0 | reduce-window | flops 2080768 | bytes 131076 | tf_op jit(solution)/shard_map/reduce-window
  1.8 0.2 slice_reduce_fusion
  2.1 0.8 fusion.3
  2.9 0.7 broadcast_add_fusion.1
  3.6 0.2 eq.78
  3.8 0.0 copy-start
  3.8 0.0 copy-start.4
  3.8 0.0 copy-start.2
  3.9 0.0 copy-start.1
  3.9 0.0 copy-start.3
  3.9 1.2 %compare_convert_fusion.send_ref = bf16[256,2048]{1,0:T(8,128)(2,1)} fusion(s32[256,2048]{1,0:T(8,128)S(1)} %bitcast.31, s32[2048]{0:T(1024)S(1)} %bitcast.34), kind=kLoop, calls=%fused_computation.1 | loop fusion | flops 1048576 | bytes 3153920 | tf_op jit(solution)/shard_map/convert_element_type | solution.py:291
  5.1 0.0 copy-done
  5.1 0.0 copy-done.4
  5.1 1.0 fusion
  6.1 0.1 reshape.73
  6.2 0.9 copy.16
  7.1 0.0 copy-done.2
  7.1 0.9 copy.13.bias_ref
  8.0 0.8 copy.12.w_in_ref
  8.8 0.7 copy.14.w_ro_ref
  9.5 20.1 %shard_map.91.runoff_ref = f32[32,512]{1,0:T(8,128)} custom-call(bf16[32,16,512]{2,1,0:T(8,128)(2,1)} %forc_ref.1, bf16[512,16]{1,0:T(8,128)(2,1)} %copy.12.w_in_ref, bf16[512,128]{1,0:T(8,128)(2,1)} %w_rec_ref.1, f32[512,1]{1,0:T(8,128)} %copy.13.bias_ref, f32[128,1]{1,0:T(8,128)} %copy.14.w_ro_ref), custom_call_target="tpu_custom_call" | custom-call | tf_op jit(solution)/shard_map/pallas_call | solution.py:80
  29.6 65.1 %shard_map.92 = f32[32,512]{1,0:T(8,128)} custom-call(f32[32,512]{1,0:T(8,128)} %shard_map.91.runoff_ref, f32[1,512]{1,0:T(1,128)} %bitcast.41, f32[1,512]{1,0:T(1,128)} %bitcast.42, bf16[256,2048]{1,0:T(8,128)(2,1)} %compare_convert_fusion.send_ref, s32[256,4]{1,0:T(8,128)} %bitcast.32), custom_call_target="tpu_custom_call" | custom-call | tf_op jit(solution)/shard_map/pallas_call | solution.py:247
  94.7 1.5 %copy.21 = f32[32,512]{1,0:T(8,128)} copy(f32[32,512]{1,0:T(8,128)} %shard_map.92) | data formatting | bytes 131072
  (9 shorter events, 0.1 us)
Async XLA Ops:
  3.8 1.3 %copy-start = (s32[512,1]{0,1:T(1,128)S(1)}, s32[512,1]{0,1:T(1,128)}, u32[]{:S(2)}) copy-start(s32[512,1]{0,1:T(1,128)} %param.16) | copy-start | bytes 6148
  3.8 1.3 %copy-start.4 = (s32[512,1]{0,1:T(1,128)S(1)}, s32[512,1]{0,1:T(1,128)}, u32[]{:S(2)}) copy-start(s32[512,1]{0,1:T(1,128)} %param.17) | copy-start | bytes 6148
  3.8 3.3 %copy-start.2 = (f32[512]{0:T(512)S(1)}, f32[512]{0:T(512)}, u32[]{:S(2)}) copy-start(f32[512]{0:T(512)} %param.12) | copy-start | bytes 6148
  3.9 4.1 %copy-start.1 = (bf16[512,16]{0,1:T(8,128)(2,1)S(1)}, bf16[512,16]{0,1:T(8,128)(2,1)}, u32[]{:S(2)}) copy-start(bf16[512,16]{0,1:T(8,128)(2,1)} %param.10) | copy-start | bytes 49156
  3.9 4.9 %copy-start.3 = (f32[128]{0:T(128)S(1)}, f32[128]{0:T(128)}, u32[]{:S(2)}) copy-start(f32[128]{0:T(128)} %param.13) | copy-start | bytes 1540

commit v10 on v8

--- a/solution.py
+++ b/solution.py
@@ -108,8 +108,9 @@
     return jnp.concatenate(day_rows, axis=0)
 
 
-def chain_kernel(n_order, n_basin, cap, runoff_ref, tt_ref, wx_ref, send_ref, tgt_ref, out_ref,
-                 packed, recv, table_ref, tgt_recv, spread, send_sem, recv_sem, tsend_sem, trecv_sem):
+def chain_kernel(n_order, n_basin, cap, runoff_ref, tt_ref, wx_ref, drains_ref, out_ref,
+                 packed, recv, table_ref, tgt_recv, spread, send_ref, tgt_ref,
+                 send_sem, recv_sem, tsend_sem, trecv_sem):
     o = lax.axis_index("order")
     b = lax.axis_index("basin")
     days, reaches = runoff_ref.shape
@@ -131,6 +132,25 @@
     @pl.when(o < n_order - 1)
     def _():
         greet(o + 1)
+
+    drain_to = drains_ref[0:1, :]
+    drain_at = drains_ref[1:2, :]
+    onehot = (lax.broadcasted_iota(jnp.int32, (n_basin, reaches), 0) == drain_to).astype(jnp.bfloat16)
+    earlier = (
+        lax.broadcasted_iota(jnp.int32, (reaches, reaches), 0)
+        < lax.broadcasted_iota(jnp.int32, (reaches, reaches), 1)
+    ).astype(jnp.bfloat16)
+    counts = jnp.dot(onehot, earlier, preferred_element_type=jnp.float32)
+    slot_index = jnp.sum(counts * onehot.astype(jnp.float32), axis=0, keepdims=True)
+    flat_slot = drain_to * cap + slot_index.astype(jnp.int32)
+    row = lax.broadcasted_iota(jnp.int32, (n_basin * rows, 1), 0)
+    row_base = lax.shift_right_logical(row, 3) * cap + jnp.bitwise_and(row, rows - 1)
+    named = (drain_at + 1).astype(jnp.float32)
+    for k in range(groups):
+        chosen = (row_base + k * rows) == flat_slot
+        send_ref[:, k * reaches : (k + 1) * reaches] = chosen.astype(jnp.bfloat16)
+        found = jnp.sum(jnp.where(chosen, named, 0.0), axis=1, keepdims=True)
+        tgt_ref[:, k : k + 1] = found.astype(jnp.int32) - 1
 
     travel = tt_ref[...]
     weight = wx_ref[...]
@@ -240,14 +260,14 @@
         lax.fori_loop(0, n_basin, finish, 0)
 
 
-def route_chain(runoff, travel_time, weight_x, send_t, tgt, n_order, n_basin, cap):
+def route_chain(runoff, travel_time, weight_x, drains, n_order, n_basin, cap):
     days, reaches = runoff.shape
     groups = cap // 8
     vmem = pl.BlockSpec(memory_space=pltpu.VMEM)
     return pl.pallas_call(
         functools.partial(chain_kernel, n_order, n_basin, cap),
         out_shape=jax.ShapeDtypeStruct((days, reaches), jnp.float32),
-        in_specs=[vmem] * 5,
+        in_specs=[vmem] * 4,
         out_specs=vmem,
         scratch_shapes=[
             pltpu.VMEM((n_basin * 8, groups * days), jnp.float32),
@@ -255,13 +275,15 @@
             pltpu.VMEM((n_basin * 8, groups * reaches), jnp.bfloat16),
             pltpu.VMEM((n_basin * 8, groups), jnp.int32),
             pltpu.VMEM((2 * groups * days, groups * reaches), jnp.bfloat16),
+            pltpu.VMEM((n_basin * 8, groups * reaches), jnp.bfloat16),
+            pltpu.VMEM((n_basin * 8, groups), jnp.int32),
             pltpu.SemaphoreType.DMA((n_basin,)),
             pltpu.SemaphoreType.DMA((n_basin,)),
             pltpu.SemaphoreType.DMA((n_basin,)),
             pltpu.SemaphoreType.DMA((n_basin,)),
         ],
         compiler_params=pltpu.CompilerParams(collective_id=0, has_side_effects=True),
-    )(runoff, travel_time.reshape(1, reaches), weight_x.reshape(1, reaches), send_t, tgt)
+    )(runoff, travel_time.reshape(1, reaches), weight_x.reshape(1, reaches), drains)
 
 
 def per_device(
@@ -269,31 +291,11 @@
 ):
     basins = lax.axis_size("basin")
     groups = lax.axis_size("order")
-    day_count = forcings.shape[0]
     reach_count = forcings.shape[2]
-    units = w_recur.shape[1]
     capacity = 2 * reach_count // basins
-    slots = basins * capacity
-    drain_to = drain_basin[:, 0]
-    onehot_drain = (drain_to[:, None] == jnp.arange(basins, dtype=jnp.int32)[None, :]).astype(
-        jnp.int32
-    )
-    slot_index = jnp.sum(jnp.cumsum(onehot_drain, axis=0) * onehot_drain, axis=1) - 1
-    flat_slot = drain_to * capacity + slot_index
-    send_int = (
-        flat_slot[:, None] == jnp.arange(slots, dtype=jnp.int32)[None, :]
-    ).astype(jnp.int32)
-    groups_k = capacity // 8
-    sent_targets = (jnp.dot(drain_reach[:, 0] + 1, send_int) - 1).reshape(basins, groups_k, 8)
-    sent_targets = sent_targets.transpose(0, 2, 1).reshape(basins * 8, groups_k)
-    send_t = (
-        jnp.arange(slots, dtype=jnp.int32)[:, None] == flat_slot[None, :]
-    ).astype(jnp.bfloat16)
-    send_t = send_t.reshape(basins, groups_k, 8, reach_count).transpose(0, 2, 1, 3)
-    send_t = send_t.reshape(basins * 8, groups_k * reach_count)
-
+    drains = jnp.stack([drain_basin[:, 0], drain_reach[:, 0]])
     runoff = lstm_runoff(forcings, w_input, w_recur, gate_bias, w_runoff)
-    return route_chain(runoff, travel_time, weight_x, send_t, sent_targets, groups, basins, capacity)
+    return route_chain(runoff, travel_time, weight_x, drains, groups, basins, capacity)
 
 
 def solution(mesh):

time: 95.1 us -> 90.3 us (0.950)
  other arithmetic: 4.6 us -> 0.6 us
  matrix products: 0.96 us -> 0 us
    convert_element_type x2 -> x0, other arithmetic: 1.91 us -> none  [the longest x1 1.22 us: per_device(): send_t = (jnp.arange(slots, dtype=jnp.int32)[:, None] == flat_slot[None,...]
    unnamed x14 -> x10, local copies, waits for them, and re-layouts: 2.27 us -> 3.57 us
    dot_general x1 -> x0, matrix products: 0.96 us -> none  [per_device(): jnp.dot(drain_reach[:, 0] + 1, send_int) - 1]
where the time goes in v10:
time: 90.3 us; the launch traced here: 90 us
  Pallas kernels  83.6 us (93%)
  local copies, waits for them, and re-layouts  5.85 us (6%)
    pallas_call x1, Pallas kernels, route_chain(): pl.pallas_call(functools.partial(chain_kernel, n_order, n_basin, cap), ou...  64.7 us
    pallas_call x1, Pallas kernels, lstm_runoff(): pl.pallas_call(functools.partial(lstm_kernel, block), out_shape=jax.Shape...  18.9 us
    unnamed x10, local copies, waits for them, and re-layouts  3.57 us

profile of v10, /device:TPU:25, one launch (start us, length us, event | category | flops | bytes accessed | tf_op | source)
XLA Modules:
  0.0 90.0 jit_solution(1184880781438036133)
XLA Ops:
  0.0 0.0 copy-start
  0.0 1.5 %copy.13.bias_ref = f32[512,1]{1,0:T(8,128)} copy(f32[512,1]{0,1:T(1,128)} %bitcast.6) | data formatting | bytes 4096 | tf_op jit(solution)/shard_map/broadcast_in_dim | solution.py:90
  1.5 0.0 copy-done
  1.5 0.8 copy.12.w_in_ref
  2.3 0.0 copy-start.3
  2.3 0.7 copy-done.3
  3.0 0.7 copy.14.w_ro_ref
  3.7 0.0 copy-start.2
  3.7 18.9 %shard_map.91.runoff_ref = f32[32,512]{1,0:T(8,128)} custom-call(bf16[32,16,512]{2,1,0:T(8,128)(2,1)} %forc_ref.1, bf16[512,16]{1,0:T(8,128)(2,1)} %copy.12.w_in_ref, bf16[512,128]{1,0:T(8,128)(2,1)} %w_rec_ref.1, f32[512,1]{1,0:T(8,128)} %copy.13.bias_ref, f32[128,1]{1,0:T(8,128)} %copy.14.w_ro_ref), custom_call_target="tpu_custom_call" | custom-call | tf_op jit(solution)/shard_map/pallas_call | solution.py:80
  22.6 0.0 copy-start.1
  22.6 0.0 copy-done.2
  22.6 0.7 copy-done.1
  23.2 0.6 pad_add_fusion.drains_ref
  23.8 64.7 %shard_map.92 = f32[32,512]{1,0:T(8,128)} custom-call(f32[32,512]{1,0:T(8,128)} %shard_map.91.runoff_ref, f32[1,512]{1,0:T(1,128)} %bitcast.7, f32[1,512]{1,0:T(1,128)} %bitcast.8, s32[2,512]{1,0:T(2,128)} %pad_add_fusion.drains_ref), custom_call_target="tpu_custom_call" | custom-call | tf_op jit(solution)/shard_map/pallas_call | solution.py:267
  88.6 1.5 %copy.16 = f32[32,512]{1,0:T(8,128)} copy(f32[32,512]{1,0:T(8,128)} %shard_map.92) | data formatting | bytes 131072
Async XLA Ops:
  0.0 1.5 %copy-start = (bf16[512,16]{0,1:T(8,128)(2,1)S(1)}, bf16[512,16]{0,1:T(8,128)(2,1)}, u32[]{:S(2)}) copy-start(bf16[512,16]{0,1:T(8,128)(2,1)} %param.10) | copy-start | bytes 49156
  2.3 0.7 copy-start.3
  3.7 18.9 %copy-start.2 = (s32[512,1]{0,1:T(1,128)S(1)}, s32[512,1]{0,1:T(1,128)}, u32[]{:S(2)}) copy-start(s32[512,1]{0,1:T(1,128)} %param.16) | copy-start | bytes 6148
  22.6 0.7 copy-start.1

commit v11 on v10

--- a/solution.py
+++ b/solution.py
@@ -99,13 +99,16 @@
 def route_days(inflow, coef):
     days = inflow.shape[0]
     c0, gain, c2 = coef
-    lagged = jnp.zeros_like(c0)
-    day_rows = []
-    for t in range(days):
-        if t > 0:
-            lagged = inflow[t - 1 : t, :] + c2 * lagged
-        day_rows.append(c0 * inflow[t : t + 1, :] + gain * lagged)
-    return jnp.concatenate(day_rows, axis=0)
+    day = lax.broadcasted_iota(jnp.int32, inflow.shape, 0)
+    lagged = jnp.where(day >= 1, pltpu.roll(inflow, shift=1, axis=0), 0.0)
+    power = c2
+    step = 1
+    while step < days:
+        moved = jnp.where(day >= step, pltpu.roll(lagged, shift=step, axis=0), 0.0)
+        lagged = lagged + power * moved
+        power = power * power
+        step *= 2
+    return c0 * inflow + gain * lagged
 
 
 def chain_kernel(n_order, n_basin, cap, runoff_ref, tt_ref, wx_ref, drains_ref, out_ref,

time: 90.3 us -> 88.9 us (0.984)
  Pallas kernels: 83.6 us -> 82.2 us
    pallas_call x1, Pallas kernels: 64.7 us -> 63.3 us  [route_chain(): pl.pallas_call(functools.partial(chain_kernel, n_order, n_basin, cap), ou...]
where the time goes in v11:
time: 88.9 us; the launch traced here: 88.7 us
  Pallas kernels  82.2 us (92%)
  local copies, waits for them, and re-layouts  5.85 us (7%)
    pallas_call x1, Pallas kernels, route_chain(): pl.pallas_call(functools.partial(chain_kernel, n_order, n_basin, cap), ou...  63.3 us
    pallas_call x1, Pallas kernels, lstm_runoff(): pl.pallas_call(functools.partial(lstm_kernel, block), out_shape=jax.Shape...  18.9 us
    unnamed x10, local copies, waits for them, and re-layouts  3.57 us

profile of v11, /device:TPU:25, one launch (start us, length us, event | category | flops | bytes accessed | tf_op | source)
XLA Modules:
  0.0 88.7 jit_solution(17997080585418465769)
XLA Ops:
  0.0 0.0 copy-start
  0.0 1.5 %copy.13.bias_ref = f32[512,1]{1,0:T(8,128)} copy(f32[512,1]{0,1:T(1,128)} %bitcast.6) | data formatting | bytes 4096 | tf_op jit(solution)/shard_map/broadcast_in_dim | solution.py:90
  1.5 0.0 copy-done
  1.5 0.8 copy.12.w_in_ref
  2.3 0.0 copy-start.3
  2.3 0.7 copy-done.3
  3.0 0.7 copy.14.w_ro_ref
  3.7 0.0 copy-start.2
  3.7 18.9 %shard_map.91.runoff_ref = f32[32,512]{1,0:T(8,128)} custom-call(bf16[32,16,512]{2,1,0:T(8,128)(2,1)} %forc_ref.1, bf16[512,16]{1,0:T(8,128)(2,1)} %copy.12.w_in_ref, bf16[512,128]{1,0:T(8,128)(2,1)} %w_rec_ref.1, f32[512,1]{1,0:T(8,128)} %copy.13.bias_ref, f32[128,1]{1,0:T(8,128)} %copy.14.w_ro_ref), custom_call_target="tpu_custom_call" | custom-call | tf_op jit(solution)/shard_map/pallas_call | solution.py:80
  22.6 0.0 copy-start.1
  22.6 0.0 copy-done.2
  22.6 0.7 copy-done.1
  23.2 0.6 pad_add_fusion.drains_ref
  23.8 63.3 %shard_map.92 = f32[32,512]{1,0:T(8,128)} custom-call(f32[32,512]{1,0:T(8,128)} %shard_map.91.runoff_ref, f32[1,512]{1,0:T(1,128)} %bitcast.7, f32[1,512]{1,0:T(1,128)} %bitcast.8, s32[2,512]{1,0:T(2,128)} %pad_add_fusion.drains_ref), custom_call_target="tpu_custom_call" | custom-call | tf_op jit(solution)/shard_map/pallas_call | solution.py:270
  87.2 1.5 %copy.16 = f32[32,512]{1,0:T(8,128)} copy(f32[32,512]{1,0:T(8,128)} %shard_map.92) | data formatting | bytes 131072
Async XLA Ops:
  0.0 1.5 %copy-start = (bf16[512,16]{0,1:T(8,128)(2,1)S(1)}, bf16[512,16]{0,1:T(8,128)(2,1)}, u32[]{:S(2)}) copy-start(bf16[512,16]{0,1:T(8,128)(2,1)} %param.10) | copy-start | bytes 49156
  2.3 0.7 copy-start.3
  3.7 18.9 %copy-start.2 = (s32[512,1]{0,1:T(1,128)S(1)}, s32[512,1]{0,1:T(1,128)}, u32[]{:S(2)}) copy-start(s32[512,1]{0,1:T(1,128)} %param.16) | copy-start | bytes 6148
  22.6 0.7 copy-start.1

commit v12 on v11

--- a/solution.py
+++ b/solution.py
@@ -38,18 +38,31 @@
     return 0.5 + 0.5 * jnp.tanh(0.5 * x)
 
 
+def as_columns(row, width):
+    hi = row.astype(jnp.bfloat16).astype(jnp.float32)
+    mid = (row - hi).astype(jnp.bfloat16).astype(jnp.float32)
+    lo = (row - hi - mid).astype(jnp.bfloat16).astype(jnp.float32)
+    parts = jnp.concatenate([hi, mid, lo, jnp.zeros((5, row.shape[1]), jnp.float32)], axis=0)
+    ones = (lax.broadcasted_iota(jnp.int32, (8, width), 0) < 3).astype(jnp.bfloat16)
+    return lax.dot_general(parts.astype(jnp.bfloat16), ones, (((0,), (0,)), ((), ())),
+                           preferred_element_type=jnp.float32)
+
+
 def lstm_kernel(block, forc_ref, w_in_ref, w_rec_ref, bias_ref, w_ro_ref, out_ref, h_scr, c_scr, run_scr):
     days = forc_ref.shape[0]
     units = w_rec_ref.shape[1]
     reaches = out_ref.shape[1]
     h_scr[...] = jnp.zeros_like(h_scr)
     c_scr[...] = jnp.zeros_like(c_scr)
+    bias = as_columns(bias_ref[...], block)
+    w_ro = as_columns(w_ro_ref[...], block)
 
     def step(t, cols):
         gates = (
-            jnp.dot(w_in_ref[...], forc_ref[t, :, cols], preferred_element_type=jnp.float32)
+            lax.dot_general(w_in_ref[...], forc_ref[t, :, cols], (((0,), (0,)), ((), ())),
+                            preferred_element_type=jnp.float32)
             + jnp.dot(w_rec_ref[...], h_scr[:, cols], preferred_element_type=jnp.float32)
-            + bias_ref[...]
+            + bias
         )
         ingate = half_tanh_sigmoid(gates[:units])
         forget = half_tanh_sigmoid(gates[units : 2 * units])
@@ -59,7 +72,7 @@
         hidden = (outgate * jnp.tanh(memory)).astype(jnp.bfloat16)
         c_scr[:, cols] = memory
         h_scr[:, cols] = hidden
-        z = jnp.sum(w_ro_ref[...] * hidden.astype(jnp.float32), axis=0, keepdims=True)
+        z = jnp.sum(w_ro * hidden.astype(jnp.float32), axis=0, keepdims=True)
         return jnp.maximum(z, 0.0) + jnp.log1p(jnp.exp(-jnp.abs(z)))
 
     def day(t, carry):
@@ -87,7 +100,7 @@
             pltpu.VMEM((units, reaches), jnp.float32),
             pltpu.VMEM((days, 1, reaches), jnp.float32),
         ],
-    )(forcings, w_input, w_recur, gate_bias[:, None], w_runoff[:, None])
+    )(forcings, w_input.T, w_recur, gate_bias.reshape(1, -1), w_runoff.reshape(1, -1))
 
 
 def split2(x):

time: 88.9 us -> 84.9 us (0.955)
  local copies, waits for them, and re-layouts: 5.85 us -> 2.17 us
    broadcast_in_dim x2 -> x0, local copies, waits for them, and re-layouts: 2.27 us -> none  [the longest x1 1.53 us: lstm_runoff(): gate_bias[:, None]]
    unnamed x10 -> x5, local copies, waits for them, and re-layouts: 3.57 us -> 2.17 us
where the time goes in v12:
time: 84.9 us; the launch traced here: 84.7 us
  Pallas kernels  81.9 us (96%)
  local copies, waits for them, and re-layouts  2.17 us (3%)
    pallas_call x1, Pallas kernels, route_chain(): pl.pallas_call(functools.partial(chain_kernel, n_order, n_basin, cap), ou...  63.3 us
    pallas_call x1, Pallas kernels, lstm_runoff(): pl.pallas_call(functools.partial(lstm_kernel, block), out_shape=jax.Shape...  18.6 us
    unnamed x5, local copies, waits for them, and re-layouts  2.17 us

profile of v12, /device:TPU:25, one launch (start us, length us, event | category | flops | bytes accessed | tf_op | source)
XLA Modules:
  0.0 84.7 jit_solution(16363495495798843467)
XLA Ops:
  0.0 0.0 copy-start.1
  0.0 0.0 copy-start
  0.0 0.7 copy-done.1
  0.7 0.0 copy-done
  0.7 0.6 pad_add_fusion.drains_ref
  1.3 18.6 %shard_map.91.runoff_ref = f32[32,512]{1,0:T(8,128)} custom-call(bf16[32,16,512]{2,1,0:T(8,128)(2,1)} %forc_ref.1, bf16[16,512]{1,0:T(8,128)(2,1)} %bitcast.7, bf16[512,128]{1,0:T(8,128)(2,1)} %w_rec_ref.1, f32[1,512]{1,0:T(1,128)} %bitcast.8, f32[1,128]{1,0:T(1,128)} %bitcast.13), custom_call_target="tpu_custom_call" | custom-call | tf_op jit(solution)/shard_map/pallas_call | solution.py:93
  19.9 63.3 %shard_map.92 = f32[32,512]{1,0:T(8,128)} custom-call(f32[32,512]{1,0:T(8,128)} %shard_map.91.runoff_ref, f32[1,512]{1,0:T(1,128)} %bitcast.9, f32[1,512]{1,0:T(1,128)} %bitcast.10, s32[2,512]{1,0:T(2,128)} %pad_add_fusion.drains_ref), custom_call_target="tpu_custom_call" | custom-call | tf_op jit(solution)/shard_map/pallas_call | solution.py:283
  83.2 1.5 %copy.11 = f32[32,512]{1,0:T(8,128)} copy(f32[32,512]{1,0:T(8,128)} %shard_map.92) | data formatting | bytes 131072
Async XLA Ops:
  0.0 0.7 copy-start.1
  0.0 0.7 copy-start

commit v13 on v12

--- a/solution.py
+++ b/solution.py
@@ -124,7 +124,7 @@
     return c0 * inflow + gain * lagged
 
 
-def chain_kernel(n_order, n_basin, cap, runoff_ref, tt_ref, wx_ref, drains_ref, out_ref,
+def chain_kernel(n_order, n_basin, cap, runoff_ref, tt_ref, wx_ref, db_ref, dr_ref, out_ref,
                  packed, recv, table_ref, tgt_recv, spread, send_ref, tgt_ref,
                  send_sem, recv_sem, tsend_sem, trecv_sem):
     o = lax.axis_index("order")
@@ -149,8 +149,8 @@
     def _():
         greet(o + 1)
 
-    drain_to = drains_ref[0:1, :]
-    drain_at = drains_ref[1:2, :]
+    drain_to = db_ref[...]
+    drain_at = dr_ref[...]
     onehot = (lax.broadcasted_iota(jnp.int32, (n_basin, reaches), 0) == drain_to).astype(jnp.bfloat16)
     earlier = (
         lax.broadcasted_iota(jnp.int32, (reaches, reaches), 0)
@@ -276,14 +276,14 @@
         lax.fori_loop(0, n_basin, finish, 0)
 
 
-def route_chain(runoff, travel_time, weight_x, drains, n_order, n_basin, cap):
+def route_chain(runoff, travel_time, weight_x, drain_basin, drain_reach, n_order, n_basin, cap):
     days, reaches = runoff.shape
     groups = cap // 8
     vmem = pl.BlockSpec(memory_space=pltpu.VMEM)
     return pl.pallas_call(
         functools.partial(chain_kernel, n_order, n_basin, cap),
         out_shape=jax.ShapeDtypeStruct((days, reaches), jnp.float32),
-        in_specs=[vmem] * 4,
+        in_specs=[vmem] * 5,
         out_specs=vmem,
         scratch_shapes=[
             pltpu.VMEM((n_basin * 8, groups * days), jnp.float32),
@@ -299,7 +299,8 @@
             pltpu.SemaphoreType.DMA((n_basin,)),
         ],
         compiler_params=pltpu.CompilerParams(collective_id=0, has_side_effects=True),
-    )(runoff, travel_time.reshape(1, reaches), weight_x.reshape(1, reaches), drains)
+    )(runoff, travel_time.reshape(1, reaches), weight_x.reshape(1, reaches),
+      drain_basin.reshape(1, reaches), drain_reach.reshape(1, reaches))
 
 
 def per_device(
@@ -309,9 +310,8 @@
     groups = lax.axis_size("order")
     reach_count = forcings.shape[2]
     capacity = 2 * reach_count // basins
-    drains = jnp.stack([drain_basin[:, 0], drain_reach[:, 0]])
     runoff = lstm_runoff(forcings, w_input, w_recur, gate_bias, w_runoff)
-    return route_chain(runoff, travel_time, weight_x, drains, groups, basins, capacity)
+    return route_chain(runoff, travel_time, weight_x, drain_basin, drain_reach, groups, basins, capacity)
 
 
 def solution(mesh):

time: 84.9 us -> 83.6 us (0.985)
    unnamed x5 -> x1, local copies, waits for them, and re-layouts: 2.17 us -> 1.47 us
where the time goes in v13:
time: 83.6 us; the launch traced here: 83.4 us
  Pallas kernels  82 us (98%)
  local copies, waits for them, and re-layouts  1.47 us (2%)
    pallas_call x1, Pallas kernels, route_chain(): pl.pallas_call(functools.partial(chain_kernel, n_order, n_basin, cap), ou...  63.4 us
    pallas_call x1, Pallas kernels, lstm_runoff(): pl.pallas_call(functools.partial(lstm_kernel, block), out_shape=jax.Shape...  18.6 us

profile of v13, /device:TPU:25, one launch (start us, length us, event | category | flops | bytes accessed | tf_op | source)
XLA Modules:
  0.0 83.4 jit_solution(828456911970457598)
XLA Ops:
  0.0 18.6 %shard_map.91.runoff_ref = f32[32,512]{1,0:T(8,128)} custom-call(bf16[32,16,512]{2,1,0:T(8,128)(2,1)} %forc_ref.1, bf16[16,512]{1,0:T(8,128)(2,1)} %bitcast.7, bf16[512,128]{1,0:T(8,128)(2,1)} %w_rec_ref.1, f32[1,512]{1,0:T(1,128)} %bitcast.8, f32[1,128]{1,0:T(1,128)} %bitcast.13), custom_call_target="tpu_custom_call" | custom-call | tf_op jit(solution)/shard_map/pallas_call | solution.py:93
  18.6 63.4 %shard_map.92 = f32[32,512]{1,0:T(8,128)} custom-call(f32[32,512]{1,0:T(8,128)} %shard_map.91.runoff_ref, f32[1,512]{1,0:T(1,128)} %bitcast.9, f32[1,512]{1,0:T(1,128)} %bitcast.10, s32[1,512]{1,0:T(1,128)} %bitcast.11, s32[1,512]{1,0:T(1,128)} %bitcast.12), custom_call_target="tpu_custom_call" | custom-call | tf_op jit(solution)/shard_map/pallas_call | solution.py:283
  82.0 1.5 %copy.11 = f32[32,512]{1,0:T(8,128)} copy(f32[32,512]{1,0:T(8,128)} %shard_map.92) | data formatting | bytes 131072

commit v14 on v13

--- a/solution.py
+++ b/solution.py
@@ -84,23 +84,6 @@
     lax.fori_loop(0, days, day, 0)
     for t in range(days):
         out_ref[t : t + 1, :] = run_scr[t]
-
-
-def lstm_runoff(forcings, w_input, w_recur, gate_bias, w_runoff, block=128):
-    days, _, reaches = forcings.shape
-    units = w_recur.shape[1]
-    vmem = pl.BlockSpec(memory_space=pltpu.VMEM)
-    return pl.pallas_call(
-        functools.partial(lstm_kernel, block),
-        out_shape=jax.ShapeDtypeStruct((days, reaches), jnp.float32),
-        in_specs=[vmem] * 5,
-        out_specs=vmem,
-        scratch_shapes=[
-            pltpu.VMEM((units, reaches), jnp.bfloat16),
-            pltpu.VMEM((units, reaches), jnp.float32),
-            pltpu.VMEM((days, 1, reaches), jnp.float32),
-        ],
-    )(forcings, w_input.T, w_recur, gate_bias.reshape(1, -1), w_runoff.reshape(1, -1))
 
 
 def split2(x):
@@ -126,7 +109,7 @@
 
 def chain_kernel(n_order, n_basin, cap, runoff_ref, tt_ref, wx_ref, db_ref, dr_ref, out_ref,
                  packed, recv, table_ref, tgt_recv, spread, send_ref, tgt_ref,
-                 send_sem, recv_sem, tsend_sem, trecv_sem):
+                 send_sem, recv_sem, tsend_sem, trecv_sem, before=None):
     o = lax.axis_index("order")
     b = lax.axis_index("basin")
     days, reaches = runoff_ref.shape
@@ -149,6 +132,8 @@
     def _():
         greet(o + 1)
 
+    if before is not None:
+        before()
     drain_to = db_ref[...]
     drain_at = dr_ref[...]
     onehot = (lax.broadcasted_iota(jnp.int32, (n_basin, reaches), 0) == drain_to).astype(jnp.bfloat16)
@@ -276,16 +261,32 @@
         lax.fori_loop(0, n_basin, finish, 0)
 
 
-def route_chain(runoff, travel_time, weight_x, drain_basin, drain_reach, n_order, n_basin, cap):
-    days, reaches = runoff.shape
+def river_kernel(block, n_order, n_basin, cap, forc_ref, w_in_ref, w_rec_ref, bias_ref, w_ro_ref,
+                 tt_ref, wx_ref, db_ref, dr_ref, out_ref, h_scr, c_scr, run_scr, runoff_ref, *rest):
+    def lstm():
+        lstm_kernel(block, forc_ref, w_in_ref, w_rec_ref, bias_ref, w_ro_ref, runoff_ref,
+                    h_scr, c_scr, run_scr)
+
+    chain_kernel(n_order, n_basin, cap, runoff_ref, tt_ref, wx_ref, db_ref, dr_ref, out_ref, *rest,
+                 before=lstm)
+
+
+def river(forcings, w_input, w_recur, gate_bias, w_runoff, travel_time, weight_x, drain_basin,
+          drain_reach, n_order, n_basin, cap, block=128):
+    days, _, reaches = forcings.shape
+    units = w_recur.shape[1]
     groups = cap // 8
     vmem = pl.BlockSpec(memory_space=pltpu.VMEM)
     return pl.pallas_call(
-        functools.partial(chain_kernel, n_order, n_basin, cap),
+        functools.partial(river_kernel, block, n_order, n_basin, cap),
         out_shape=jax.ShapeDtypeStruct((days, reaches), jnp.float32),
-        in_specs=[vmem] * 5,
+        in_specs=[vmem] * 9,
         out_specs=vmem,
         scratch_shapes=[
+            pltpu.VMEM((units, reaches), jnp.bfloat16),
+            pltpu.VMEM((units, reaches), jnp.float32),
+            pltpu.VMEM((days, 1, reaches), jnp.float32),
+            pltpu.VMEM((days, reaches), jnp.float32),
             pltpu.VMEM((n_basin * 8, groups * days), jnp.float32),
             pltpu.VMEM((n_basin * 8, groups * days), jnp.float32),
             pltpu.VMEM((n_basin * 8, groups * reaches), jnp.bfloat16),
@@ -299,7 +300,8 @@
             pltpu.SemaphoreType.DMA((n_basin,)),
         ],
         compiler_params=pltpu.CompilerParams(collective_id=0, has_side_effects=True),
-    )(runoff, travel_time.reshape(1, reaches), weight_x.reshape(1, reaches),
+    )(forcings, w_input.T, w_recur, gate_bias.reshape(1, -1), w_runoff.reshape(1, -1),
+      travel_time.reshape(1, reaches), weight_x.reshape(1, reaches),
       drain_basin.reshape(1, reaches), drain_reach.reshape(1, reaches))
 
 
@@ -310,8 +312,8 @@
     groups = lax.axis_size("order")
     reach_count = forcings.shape[2]
     capacity = 2 * reach_count // basins
-    runoff = lstm_runoff(forcings, w_input, w_recur, gate_bias, w_runoff)
-    return route_chain(runoff, travel_time, weight_x, drain_basin, drain_reach, groups, basins, capacity)
+    return river(forcings, w_input, w_recur, gate_bias, w_runoff, travel_time, weight_x,
+                 drain_basin, drain_reach, groups, basins, capacity)
 
 
 def solution(mesh):

time: 83.6 us -> 79.4 us (0.950)
  Pallas kernels: 82 us -> 77.8 us
    pallas_call x2 -> x1, Pallas kernels: 82 us -> 77.8 us  [river(): pl.pallas_call(functools.partial(river_kernel, block, n_order, n_basin, c...]
where the time goes in v14:
time: 79.4 us; the launch traced here: 79.3 us
  Pallas kernels  77.8 us (98%)
  local copies, waits for them, and re-layouts  1.47 us (2%)
    pallas_call x1, Pallas kernels, river(): pl.pallas_call(functools.partial(river_kernel, block, n_order, n_basin, c...  77.8 us

profile of v14, /device:TPU:25, one launch (start us, length us, event | category | flops | bytes accessed | tf_op | source)
XLA Modules:
  0.0 79.3 jit_solution(953338760076440094)
XLA Ops:
  0.0 77.8 %shard_map.91 = f32[32,512]{1,0:T(8,128)} custom-call(bf16[32,16,512]{2,1,0:T(8,128)(2,1)} %forc_ref.1, bf16[16,512]{1,0:T(8,128)(2,1)} %bitcast.7, bf16[512,128]{1,0:T(8,128)(2,1)} %w_rec_ref.1, f32[1,512]{1,0:T(1,128)} %bitcast.8, f32[1,128]{1,0:T(1,128)} %bitcast.13, f32[1,512]{1,0:T(1,128)} %bitcast.9, f32[1,512]{1,0:T(1,128)} %bitcast.10, ...), custom_call_target="tpu_custom_call" | custom-call | tf_op jit(solution)/shard_map/pallas_call | solution.py:280
  77.8 1.5 %copy.11 = f32[32,512]{1,0:T(8,128)} copy(f32[32,512]{1,0:T(8,128)} %shard_map.91) | data formatting | bytes 131072

commit v15 on v14

--- a/solution.py
+++ b/solution.py
@@ -173,12 +173,6 @@
 
     spread[...] = jnp.zeros_like(spread)
 
-    @pl.when(o == 0)
-    def _():
-        discharge = route_days(runoff_ref[...], coef)
-        out_ref[...] = discharge
-        pack(discharge)
-
     at_end = jnp.logical_or(o == 0, o == n_order - 1)
 
     @pl.when(at_end)
@@ -215,6 +209,12 @@
             target_copy(j, b, o + 1).start()
             return carry
         lax.fori_loop(0, n_basin, start, 0)
+
+    @pl.when(o == 0)
+    def _():
+        discharge = route_days(runoff_ref[...], coef)
+        out_ref[...] = discharge
+        pack(discharge)
 
     @pl.when(o > 0)
     def _():

time: 79.4 us -> 79.4 us (level)
  no operation moved by 1% of the time
where the time goes in v15:
time: 79.4 us; the launch traced here: 79.3 us
  Pallas kernels  77.8 us (98%)
  local copies, waits for them, and re-layouts  1.47 us (2%)
    pallas_call x1, Pallas kernels, river(): pl.pallas_call(functools.partial(river_kernel, block, n_order, n_basin, c...  77.8 us

profile of v15, /device:TPU:25, one launch (start us, length us, event | category | flops | bytes accessed | tf_op | source)
XLA Modules:
  0.0 79.3 jit_solution(2470376378430848517)
XLA Ops:
  0.0 77.8 %shard_map.91 = f32[32,512]{1,0:T(8,128)} custom-call(bf16[32,16,512]{2,1,0:T(8,128)(2,1)} %forc_ref.1, bf16[16,512]{1,0:T(8,128)(2,1)} %bitcast.7, bf16[512,128]{1,0:T(8,128)(2,1)} %w_rec_ref.1, f32[1,512]{1,0:T(1,128)} %bitcast.8, f32[1,128]{1,0:T(1,128)} %bitcast.13, f32[1,512]{1,0:T(1,128)} %bitcast.9, f32[1,512]{1,0:T(1,128)} %bitcast.10, ...), custom_call_target="tpu_custom_call" | custom-call | tf_op jit(solution)/shard_map/pallas_call | solution.py:280
  77.8 1.5 %copy.11 = f32[32,512]{1,0:T(8,128)} copy(f32[32,512]{1,0:T(8,128)} %shard_map.91) | data formatting | bytes 131072

commit v16 on v15

--- a/solution.py
+++ b/solution.py
@@ -272,7 +272,7 @@
 
 
 def river(forcings, w_input, w_recur, gate_bias, w_runoff, travel_time, weight_x, drain_basin,
-          drain_reach, n_order, n_basin, cap, block=128):
+          drain_reach, n_order, n_basin, cap, block=64):
     days, _, reaches = forcings.shape
     units = w_recur.shape[1]
     groups = cap // 8

time: 79.4 us -> 104 us (1.31)
  Pallas kernels: 77.8 us -> 102 us
    pallas_call x1, Pallas kernels: 77.8 us -> 102 us  [river(): pl.pallas_call(functools.partial(river_kernel, block, n_order, n_basin, c...]
where the time goes in v16:
time: 104 us; the launch traced here: 103 us
  Pallas kernels  102 us (98%)
  local copies, waits for them, and re-layouts  1.47 us (1%)
    pallas_call x1, Pallas kernels, river(): pl.pallas_call(functools.partial(river_kernel, block, n_order, n_basin, c...  102 us

profile of v16, /device:TPU:25, one launch (start us, length us, event | category | flops | bytes accessed | tf_op | source)
XLA Modules:
  0.0 103.4 jit_solution(14217727036603058752)
XLA Ops:
  0.0 101.9 %shard_map.91 = f32[32,512]{1,0:T(8,128)} custom-call(bf16[32,16,512]{2,1,0:T(8,128)(2,1)} %forc_ref.1, bf16[16,512]{1,0:T(8,128)(2,1)} %bitcast.7, bf16[512,128]{1,0:T(8,128)(2,1)} %w_rec_ref.1, f32[1,512]{1,0:T(1,128)} %bitcast.8, f32[1,128]{1,0:T(1,128)} %bitcast.13, f32[1,512]{1,0:T(1,128)} %bitcast.9, f32[1,512]{1,0:T(1,128)} %bitcast.10, ...), custom_call_target="tpu_custom_call" | custom-call | tf_op jit(solution)/shard_map/pallas_call | solution.py:280
  101.9 1.5 %copy.11 = f32[32,512]{1,0:T(8,128)} copy(f32[32,512]{1,0:T(8,128)} %shard_map.91) | data formatting | bytes 131072

commit v17 on v15

--- a/solution.py
+++ b/solution.py
@@ -232,14 +232,13 @@
             data_copy(j, j, o - 1).wait_recv()
             return carry
         lax.fori_loop(0, n_basin, arrived, 0)
-        both = jnp.concatenate(split2(recv[...]), axis=1)
-        stacked = lax.dot_general(both, table_ref[...], (((0,), (0,)), ((), ())),
-                                  preferred_element_type=jnp.float32)
-        half = stacked.shape[0] // 2
-        wide = stacked[:half] + stacked[half:]
-        arrive = wide[0:days, 0:reaches]
-        for k in range(1, groups):
-            arrive = arrive + wide[k * days : (k + 1) * days, k * reaches : (k + 1) * reaches]
+        arrive = None
+        for k in range(groups):
+            block = jnp.concatenate(split2(recv[:, k * days : (k + 1) * days]), axis=1)
+            term = lax.dot_general(block, table_ref[:, k * reaches : (k + 1) * reaches],
+                                   (((0,), (0,)), ((), ())), preferred_element_type=jnp.float32)
+            term = term[:days] + term[days:]
+            arrive = term if arrive is None else arrive + term
         discharge = route_days(runoff_ref[...] + arrive, coef)
         out_ref[...] = discharge
 

time: 79.4 us -> 79.4 us (level)
  no operation moved by 1% of the time
where the time goes in v17:
time: 79.4 us; the launch traced here: 79.2 us
  Pallas kernels  77.7 us (98%)
  local copies, waits for them, and re-layouts  1.47 us (2%)
    pallas_call x1, Pallas kernels, river(): pl.pallas_call(functools.partial(river_kernel, block, n_order, n_basin, c...  77.7 us

profile of v17, /device:TPU:25, one launch (start us, length us, event | category | flops | bytes accessed | tf_op | source)
XLA Modules:
  0.0 79.2 jit_solution(5575204364233706121)
XLA Ops:
  0.0 77.7 %shard_map.91 = f32[32,512]{1,0:T(8,128)} custom-call(bf16[32,16,512]{2,1,0:T(8,128)(2,1)} %forc_ref.1, bf16[16,512]{1,0:T(8,128)(2,1)} %bitcast.7, bf16[512,128]{1,0:T(8,128)(2,1)} %w_rec_ref.1, f32[1,512]{1,0:T(1,128)} %bitcast.8, f32[1,128]{1,0:T(1,128)} %bitcast.13, f32[1,512]{1,0:T(1,128)} %bitcast.9, f32[1,512]{1,0:T(1,128)} %bitcast.10, ...), custom_call_target="tpu_custom_call" | custom-call | tf_op jit(solution)/shard_map/pallas_call | solution.py:279
  77.7 1.5 %copy.11 = f32[32,512]{1,0:T(8,128)} copy(f32[32,512]{1,0:T(8,128)} %shard_map.91) | data formatting | bytes 131072

commit v18 on v17

--- a/solution.py
+++ b/solution.py
@@ -206,7 +206,7 @@
     @pl.when(o < n_order - 1)
     def _():
         def start(j, carry):
-            target_copy(j, b, o + 1).start()
+            target_copy(lax.rem(b + j, n_basin), b, o + 1).start()
             return carry
         lax.fori_loop(0, n_basin, start, 0)
 
@@ -249,7 +249,7 @@
     @pl.when(o < n_order - 1)
     def _():
         def start(j, carry):
-            data_copy(j, b, o + 1).start()
+            data_copy(lax.rem(b + j, n_basin), b, o + 1).start()
             return carry
         lax.fori_loop(0, n_basin, start, 0)
 

time: 79.4 us -> 82.5 us (1.039)
  Pallas kernels: 77.7 us -> 80.9 us
    pallas_call x1, Pallas kernels: 77.7 us -> 80.9 us  [river(): pl.pallas_call(functools.partial(river_kernel, block, n_order, n_basin, c...]
where the time goes in v18:
time: 82.5 us; the launch traced here: 82.4 us
  Pallas kernels  80.9 us (98%)
  local copies, waits for them, and re-layouts  1.47 us (2%)
    pallas_call x1, Pallas kernels, river(): pl.pallas_call(functools.partial(river_kernel, block, n_order, n_basin, c...  80.9 us

profile of v18, /device:TPU:25, one launch (start us, length us, event | category | flops | bytes accessed | tf_op | source)
XLA Modules:
  0.0 82.4 jit_solution(15781332139502746070)
XLA Ops:
  0.0 80.9 %shard_map.91 = f32[32,512]{1,0:T(8,128)} custom-call(bf16[32,16,512]{2,1,0:T(8,128)(2,1)} %forc_ref.1, bf16[16,512]{1,0:T(8,128)(2,1)} %bitcast.7, bf16[512,128]{1,0:T(8,128)(2,1)} %w_rec_ref.1, f32[1,512]{1,0:T(1,128)} %bitcast.8, f32[1,128]{1,0:T(1,128)} %bitcast.13, f32[1,512]{1,0:T(1,128)} %bitcast.9, f32[1,512]{1,0:T(1,128)} %bitcast.10, ...), custom_call_target="tpu_custom_call" | custom-call | tf_op jit(solution)/shard_map/pallas_call | solution.py:279
  80.9 1.5 %copy.11 = f32[32,512]{1,0:T(8,128)} copy(f32[32,512]{1,0:T(8,128)} %shard_map.91) | data formatting | bytes 131072

commit v19 on v18

--- a/solution.py
+++ b/solution.py
@@ -206,7 +206,7 @@
     @pl.when(o < n_order - 1)
     def _():
         def start(j, carry):
-            target_copy(lax.rem(b + j, n_basin), b, o + 1).start()
+            target_copy(lax.rem(b + n_basin // 2 + j, n_basin), b, o + 1).start()
             return carry
         lax.fori_loop(0, n_basin, start, 0)
 
@@ -249,7 +249,7 @@
     @pl.when(o < n_order - 1)
     def _():
         def start(j, carry):
-            data_copy(lax.rem(b + j, n_basin), b, o + 1).start()
+            data_copy(lax.rem(b + n_basin // 2 + j, n_basin), b, o + 1).start()
             return carry
         lax.fori_loop(0, n_basin, start, 0)
 

time: 82.5 us -> 81.4 us (0.987)
  Pallas kernels: 80.9 us -> 79.8 us
    pallas_call x1, Pallas kernels: 80.9 us -> 79.8 us  [river(): pl.pallas_call(functools.partial(river_kernel, block, n_order, n_basin, c...]
where the time goes in v19:
time: 81.4 us; the launch traced here: 81.3 us
  Pallas kernels  79.8 us (98%)
  local copies, waits for them, and re-layouts  1.47 us (2%)
    pallas_call x1, Pallas kernels, river(): pl.pallas_call(functools.partial(river_kernel, block, n_order, n_basin, c...  79.8 us

profile of v19, /device:TPU:25, one launch (start us, length us, event | category | flops | bytes accessed | tf_op | source)
XLA Modules:
  0.0 81.3 jit_solution(9275484670178141468)
XLA Ops:
  0.0 79.8 %shard_map.91 = f32[32,512]{1,0:T(8,128)} custom-call(bf16[32,16,512]{2,1,0:T(8,128)(2,1)} %forc_ref.1, bf16[16,512]{1,0:T(8,128)(2,1)} %bitcast.7, bf16[512,128]{1,0:T(8,128)(2,1)} %w_rec_ref.1, f32[1,512]{1,0:T(1,128)} %bitcast.8, f32[1,128]{1,0:T(1,128)} %bitcast.13, f32[1,512]{1,0:T(1,128)} %bitcast.9, f32[1,512]{1,0:T(1,128)} %bitcast.10, ...), custom_call_target="tpu_custom_call" | custom-call | tf_op jit(solution)/shard_map/pallas_call | solution.py:279
  79.8 1.5 %copy.11 = f32[32,512]{1,0:T(8,128)} copy(f32[32,512]{1,0:T(8,128)} %shard_map.91) | data formatting | bytes 131072

commit v20 on v17

--- a/solution.py
+++ b/solution.py
@@ -147,10 +147,16 @@
     row = lax.broadcasted_iota(jnp.int32, (n_basin * rows, 1), 0)
     row_base = lax.shift_right_logical(row, 3) * cap + jnp.bitwise_and(row, rows - 1)
     named = (drain_at + 1).astype(jnp.float32)
+    named_hi, named_lo = split2(named)
+    named_parts = jnp.concatenate(
+        [named_hi.astype(jnp.float32), named_lo.astype(jnp.float32),
+         jnp.zeros((6, reaches), jnp.float32)], axis=0).astype(jnp.bfloat16)
     for k in range(groups):
-        chosen = (row_base + k * rows) == flat_slot
-        send_ref[:, k * reaches : (k + 1) * reaches] = chosen.astype(jnp.bfloat16)
-        found = jnp.sum(jnp.where(chosen, named, 0.0), axis=1, keepdims=True)
+        chosen = ((row_base + k * rows) == flat_slot).astype(jnp.bfloat16)
+        send_ref[:, k * reaches : (k + 1) * reaches] = chosen
+        picked = lax.dot_general(chosen, named_parts, (((1,), (1,)), ((), ())),
+                                 preferred_element_type=jnp.float32)
+        found = picked[:, 0:1] + picked[:, 1:2]
         tgt_ref[:, k : k + 1] = found.astype(jnp.int32) - 1
 
     travel = tt_ref[...]

time: 79.4 us -> 79.7 us (level)
  no operation moved by 1% of the time
where the time goes in v20:
time: 79.7 us; the launch traced here: 79.5 us
  Pallas kernels  78.1 us (98%)
  local copies, waits for them, and re-layouts  1.47 us (2%)
    pallas_call x1, Pallas kernels, river(): pl.pallas_call(functools.partial(river_kernel, block, n_order, n_basin, c...  78.1 us

profile of v20, /device:TPU:25, one launch (start us, length us, event | category | flops | bytes accessed | tf_op | source)
XLA Modules:
  0.0 79.5 jit_solution(1948652433077626810)
XLA Ops:
  0.0 78.1 %shard_map.91 = f32[32,512]{1,0:T(8,128)} custom-call(bf16[32,16,512]{2,1,0:T(8,128)(2,1)} %forc_ref.1, bf16[16,512]{1,0:T(8,128)(2,1)} %bitcast.7, bf16[512,128]{1,0:T(8,128)(2,1)} %w_rec_ref.1, f32[1,512]{1,0:T(1,128)} %bitcast.8, f32[1,128]{1,0:T(1,128)} %bitcast.13, f32[1,512]{1,0:T(1,128)} %bitcast.9, f32[1,512]{1,0:T(1,128)} %bitcast.10, ...), custom_call_target="tpu_custom_call" | custom-call | tf_op jit(solution)/shard_map/pallas_call | solution.py:285
  78.1 1.5 %copy.11 = f32[32,512]{1,0:T(8,128)} copy(f32[32,512]{1,0:T(8,128)} %shard_map.91) | data formatting | bytes 131072
